TPU v7x, 32 devices: a whole 2x2x4 slice. The times are simulated.
32 devices in a mesh: rep: 8 (over y, x, core), fsdp: 4 (over z).
Axes of the slice: x: 2, y: 2, z: 4, core: 2. Of those that a mesh axis runs over, the one named last changes fastest.
Arguments:
- tokens: bfloat16 [8192, 1024], P(('rep', 'fsdp')), may hold values from -6 to 6
- doc_lengths: int32 [32, 8], P(('rep', 'fsdp')), may hold values from 0 to 256, as said below
- attn_norm: bfloat16 [1024], P('fsdp'), may hold values from 0.5 to 1.5
- w_query: bfloat16 [1024, 2048], P('fsdp'), may hold values from -0.1875 to 0.1875
- key_matrix: bfloat16 [1024, 1024], P('fsdp'), may hold values from -0.1875 to 0.1875
- value_matrix: bfloat16 [1024, 1024], P('fsdp'), may hold values from -0.1875 to 0.1875
- head_norms: bfloat16 [2, 128], replicated, may hold values from 0.25 to 1.75
- w_out: bfloat16 [2048, 1024], P('fsdp'), may hold values from -0.5 to 0.5
- ffn_norm: bfloat16 [1024], P('fsdp'), may hold values from 0.5 to 1.5
- w_gate: bfloat16 [1024, 3072], P('fsdp'), may hold values from -0.1875 to 0.1875
- w_up: bfloat16 [1024, 3072], P('fsdp'), may hold values from -0.1875 to 0.1875
- w_down: bfloat16 [3072, 1024], P('fsdp'), may hold values from -0.109375 to 0.109375
- cotangent: bfloat16 [8192, 1024], P(('rep', 'fsdp')), may hold values from -6 to 6
Outputs:
- mixed: bfloat16 [8192, 1024], P(('rep', 'fsdp'))
- d_tokens: bfloat16 [8192, 1024], P(('rep', 'fsdp'))
- d_attn_norm: float32 [1024], P('fsdp')
- d_w_query: float32 [1024, 2048], P('fsdp')
- d_w_key: float32 [1024, 1024], P('fsdp')
- d_w_value: float32 [1024, 1024], P('fsdp')
- d_head_norms: float32 [2, 128], replicated
- d_w_out: float32 [2048, 1024], P('fsdp')
- d_ffn_norm: float32 [1024], P('fsdp')
- d_w_gate: float32 [1024, 3072], P('fsdp')
- d_w_up: float32 [1024, 3072], P('fsdp')
- d_w_down: float32 [3072, 1024], P('fsdp')
Inputs may be any that keep to these rules, and one draw needn't show every extreme that they name: `doc_lengths`: row j lists the sequences packed from the first token row of device block j onward; zeros are empty slots; each row sums to 128 or more and to 256 or less; in every draw some device holds one sequence of 256 tokens.
All inputs are finite; a program needn't handle non-finite values.
Results may differ from a plain program's by a relative error of at most 0.02.
Values may be sent and summed in bfloat16 or wider, within the bound.
A program may use at most 192 MiB of HBM per device.

v0:
```python
import math

import jax
import jax.numpy as jnp
from jax import lax
from jax.sharding import PartitionSpec as P

QUERY_HEADS = 16
KEY_VALUE_HEADS = 8
HEAD_WIDTH = 128


EPS = 1e-06
ROPE_BASE = 1000000.0
NEG_FILL = -1e30


def layout(lengths, count_of_rows):
    seq_ends = jnp.cumsum(lengths)
    seq_starts = seq_ends - lengths
    row_ids = jnp.arange(count_of_rows, dtype=jnp.int32)
    segment = jnp.sum((row_ids[:, None] >= seq_ends[None, :]).astype(jnp.int32), axis=1)
    slot_ids = jnp.arange(lengths.shape[0], dtype=jnp.int32)
    member = (segment[:, None] == slot_ids[None, :]).astype(jnp.int32)
    position = row_ids - jnp.sum(member * seq_starts[None, :], axis=1)
    live_rows = row_ids < seq_ends[-1]
    causal = (
        (segment[:, None] == segment[None, :])
        & (row_ids[None, :] <= row_ids[:, None])
        & live_rows[:, None]
    )
    allowed = causal | (row_ids[:, None] == row_ids[None, :])
    return (position, live_rows, allowed)


def rope_tables(position, width):
    half_width = width // 2
    index = jnp.arange(half_width, dtype=jnp.float32)
    freq_table = jnp.exp(index * (-2.0 * math.log(ROPE_BASE) / width))
    angle = position.astype(jnp.float32)[:, None] * freq_table[None, :]
    return (jnp.cos(angle), jnp.sin(angle))


def apply_rotation(values_in, cosine_table, sine_table):
    half_width = values_in.shape[-1] // 2
    first_half = values_in[..., :half_width]
    second_half = values_in[..., half_width:]
    cos_rows = cosine_table[:, None, :]
    sin_rows = sine_table[:, None, :]
    return jnp.concatenate(
        [
            first_half * cos_rows - second_half * sin_rows,
            second_half * cos_rows + first_half * sin_rows,
        ],
        axis=-1,
    )


def rows_product(left, right):
    return lax.dot_general(
        left, right, (((0,), (0,)), ((), ())), preferred_element_type=jnp.float32
    )


def cols_product(left, right):
    return lax.dot_general(
        left, right, (((1,), (1,)), ((), ())), preferred_element_type=jnp.float32
    )


def norm_back(grad_in, hat_rows, row_scale, gain_full):
    leading_axes = tuple(range(grad_in.ndim - 1))
    grad_gain = jnp.sum(grad_in * hat_rows, axis=leading_axes)
    scaled_grad = grad_in * gain_full
    centered = scaled_grad - hat_rows * jnp.mean(scaled_grad * hat_rows, axis=-1, keepdims=True)
    return (row_scale * centered, grad_gain)


def head_stats(values_in):
    head_scale = lax.rsqrt(jnp.mean(values_in * values_in, axis=2, keepdims=True) + EPS)
    return (values_in * head_scale, head_scale)


def per_device(
    tokens,
    doc_lengths,
    attn_norm,
    w_query,
    key_matrix,
    value_matrix,
    head_norms,
    w_out,
    ffn_norm,
    w_gate,
    w_up,
    w_down,
    cotangent,
):
    count_of_rows = tokens.shape[0]
    group_width = QUERY_HEADS // KEY_VALUE_HEADS
    score_scale = HEAD_WIDTH ** (-0.5)
    fsdp_count = lax.axis_size("fsdp")
    rep_count = lax.axis_size("rep")
    position, live_rows, allowed = layout(doc_lengths[0], count_of_rows)
    cosine_table, sine_table = rope_tables(position, HEAD_WIDTH)
    head_gains = head_norms.astype(jnp.float32)
    query_full, key_full, value_full, out_full, norm_one = (
        lax.all_gather(w_query, "fsdp", axis=0, tiled=True),
        lax.all_gather(key_matrix, "fsdp", axis=0, tiled=True),
        lax.all_gather(value_matrix, "fsdp", axis=0, tiled=True),
        lax.all_gather(w_out, "fsdp", axis=0, tiled=True),
        lax.all_gather(attn_norm, "fsdp", axis=0, tiled=True),
    )
    inputs = tokens.astype(jnp.float32)
    first_scale = lax.rsqrt(jnp.mean(inputs * inputs, axis=1, keepdims=True) + EPS)
    first_hat = inputs * first_scale
    normalized_rows = (first_hat * norm_one).astype(jnp.bfloat16)
    query = jnp.dot(normalized_rows, query_full, preferred_element_type=jnp.float32).reshape(
        count_of_rows, QUERY_HEADS, HEAD_WIDTH
    )
    keys_before_rotation = jnp.dot(
        normalized_rows, key_full, preferred_element_type=jnp.float32
    ).reshape(count_of_rows, KEY_VALUE_HEADS, HEAD_WIDTH)
    value_rows = jnp.dot(normalized_rows, value_full, preferred_element_type=jnp.float32).astype(
        jnp.bfloat16
    )
    query_hat, query_scale = head_stats(query)
    key_hat, key_scale = head_stats(keys_before_rotation)
    rotated_query = apply_rotation(query_hat * head_gains[0], cosine_table, sine_table).astype(
        jnp.bfloat16
    )
    key_rot = apply_rotation(key_hat * head_gains[1], cosine_table, sine_table).astype(jnp.bfloat16)
    query_head_rows = jnp.moveaxis(
        rotated_query.reshape(count_of_rows, KEY_VALUE_HEADS, group_width, HEAD_WIDTH), 1, 0
    )
    key_heads = jnp.moveaxis(key_rot, 1, 0)
    value_head_rows = jnp.moveaxis(
        value_rows.reshape(count_of_rows, KEY_VALUE_HEADS, HEAD_WIDTH), 1, 0
    )

    def masked_scores(query_j, key_j):
        scores = (
            jnp.einsum("tgd,sd->gts", query_j, key_j, preferred_element_type=jnp.float32)
            * score_scale
        )
        return jnp.where(allowed[None], scores, NEG_FILL)

    def attend(parts):
        query_j, key_j, value_j = parts
        scores = masked_scores(query_j, key_j)
        highest = jnp.max(scores, axis=2, keepdims=True)
        expd = jnp.exp(scores - highest)
        totals = jnp.sum(expd, axis=2, keepdims=True)
        probs = (expd / totals).astype(jnp.bfloat16)
        head_out = jnp.einsum("gts,sd->tgd", probs, value_j, preferred_element_type=jnp.float32)
        return (head_out.astype(jnp.bfloat16), (highest + jnp.log(totals))[..., 0])

    mixed_heads, lse_heads = lax.map(attend, (query_head_rows, key_heads, value_head_rows))
    attended = jnp.moveaxis(mixed_heads, 0, 1).reshape(count_of_rows, QUERY_HEADS * HEAD_WIDTH)
    hidden = inputs + jnp.dot(attended, out_full, preferred_element_type=jnp.float32)
    gate_full, up_full, down_full, norm_two = (
        lax.all_gather(w_gate, "fsdp", axis=0, tiled=True),
        lax.all_gather(w_up, "fsdp", axis=0, tiled=True),
        lax.all_gather(w_down, "fsdp", axis=0, tiled=True),
        lax.all_gather(ffn_norm, "fsdp", axis=0, tiled=True),
    )
    second_scale = lax.rsqrt(jnp.mean(hidden * hidden, axis=1, keepdims=True) + EPS)
    second_hat = hidden * second_scale
    normed_two = (second_hat * norm_two).astype(jnp.bfloat16)
    gate = jnp.dot(normed_two, gate_full, preferred_element_type=jnp.float32)
    up_part = jnp.dot(normed_two, up_full, preferred_element_type=jnp.float32)
    sigma = jax.nn.sigmoid(gate)
    activated = (gate * sigma * up_part).astype(jnp.bfloat16)
    output = hidden + jnp.dot(activated, down_full, preferred_element_type=jnp.float32)
    mixed = jnp.where(live_rows[:, None], output, 0.0).astype(jnp.bfloat16)
    gate_full, up_full, down_full, norm_two = (
        lax.all_gather(w_gate, "fsdp", axis=0, tiled=True),
        lax.all_gather(w_up, "fsdp", axis=0, tiled=True),
        lax.all_gather(w_down, "fsdp", axis=0, tiled=True),
        lax.all_gather(ffn_norm, "fsdp", axis=0, tiled=True),
    )
    d_output = jnp.where(live_rows[:, None], cotangent.astype(jnp.float32), 0.0)
    d_branch = d_output.astype(jnp.bfloat16)
    grad_down = rows_product(activated, d_branch)
    d_activated = cols_product(d_branch, down_full)
    d_gate = (d_activated * up_part * sigma * (1.0 + gate * (1.0 - sigma))).astype(jnp.bfloat16)
    d_up = (d_activated * gate * sigma).astype(jnp.bfloat16)
    grad_gate = rows_product(normed_two, d_gate)
    grad_up = rows_product(normed_two, d_up)
    d_normed_two = cols_product(d_gate, gate_full) + cols_product(d_up, up_full)
    d_hidden_norm, grad_norm_two = norm_back(d_normed_two, second_hat, second_scale, norm_two)
    d_hidden = d_output + d_hidden_norm
    ffn_shards = (
        lax.psum_scatter(
            grad_gate.astype(jnp.bfloat16), "fsdp", scatter_dimension=0, tiled=True
        ).astype(jnp.float32),
        lax.psum_scatter(
            grad_up.astype(jnp.bfloat16), "fsdp", scatter_dimension=0, tiled=True
        ).astype(jnp.float32),
        lax.psum_scatter(
            grad_down.astype(jnp.bfloat16), "fsdp", scatter_dimension=0, tiled=True
        ).astype(jnp.float32),
        lax.psum_scatter(
            grad_norm_two.astype(jnp.bfloat16), "fsdp", scatter_dimension=0, tiled=True
        ).astype(jnp.float32),
    )
    ffn_sums = (
        lax.psum(ffn_shards[0].astype(jnp.bfloat16), "rep").astype(jnp.float32),
        lax.psum(ffn_shards[1].astype(jnp.bfloat16), "rep").astype(jnp.float32),
        lax.psum(ffn_shards[2].astype(jnp.bfloat16), "rep").astype(jnp.float32),
        lax.psum(ffn_shards[3].astype(jnp.bfloat16), "rep").astype(jnp.float32),
    )
    query_full, key_full, value_full, out_full, norm_one = (
        lax.all_gather(w_query, "fsdp", axis=0, tiled=True),
        lax.all_gather(key_matrix, "fsdp", axis=0, tiled=True),
        lax.all_gather(value_matrix, "fsdp", axis=0, tiled=True),
        lax.all_gather(w_out, "fsdp", axis=0, tiled=True),
        lax.all_gather(attn_norm, "fsdp", axis=0, tiled=True),
    )
    d_attn = d_hidden.astype(jnp.bfloat16)
    grad_out = rows_product(attended, d_attn)
    attended_gradient = cols_product(d_attn, out_full).astype(jnp.bfloat16)
    head_gradients = jnp.moveaxis(
        attended_gradient.reshape(count_of_rows, KEY_VALUE_HEADS, group_width, HEAD_WIDTH), 1, 0
    )

    def attend_back(parts):
        query_j, key_j, value_j, grad_j, lse_j = parts
        scores = masked_scores(query_j, key_j)
        probs = jnp.exp(scores - lse_j[..., None])
        d_probs = jnp.einsum("tgd,sd->gts", grad_j, value_j, preferred_element_type=jnp.float32)
        center = jnp.sum(probs * d_probs, axis=2, keepdims=True)
        d_scores = (probs * (d_probs - center)).astype(jnp.bfloat16)
        d_value_j = jnp.einsum(
            "gts,tgd->sd", probs.astype(jnp.bfloat16), grad_j, preferred_element_type=jnp.float32
        )
        d_query_j = (
            jnp.einsum("gts,sd->tgd", d_scores, key_j, preferred_element_type=jnp.float32)
            * score_scale
        )
        d_key_j = (
            jnp.einsum("gts,tgd->sd", d_scores, query_j, preferred_element_type=jnp.float32)
            * score_scale
        )
        return (d_query_j, d_key_j, d_value_j)

    d_query_heads, d_key_heads, value_head_gradient = lax.map(
        attend_back, (query_head_rows, key_heads, value_head_rows, head_gradients, lse_heads)
    )
    d_query_rot = jnp.moveaxis(d_query_heads, 0, 1).reshape(count_of_rows, QUERY_HEADS, HEAD_WIDTH)
    rotated_key_gradient = jnp.moveaxis(d_key_heads, 0, 1)
    query_norm_grad = apply_rotation(d_query_rot, cosine_table, -sine_table)
    key_norm_grad = apply_rotation(rotated_key_gradient, cosine_table, -sine_table)
    query_pre_grad, grad_query_gain = norm_back(
        query_norm_grad, query_hat, query_scale, head_gains[0]
    )
    key_pre_grad, grad_key_gain = norm_back(key_norm_grad, key_hat, key_scale, head_gains[1])
    d_query = query_pre_grad.reshape(count_of_rows, QUERY_HEADS * HEAD_WIDTH).astype(jnp.bfloat16)
    key_gradient = key_pre_grad.reshape(count_of_rows, KEY_VALUE_HEADS * HEAD_WIDTH).astype(
        jnp.bfloat16
    )
    value_gradient = (
        jnp.moveaxis(value_head_gradient, 0, 1)
        .reshape(count_of_rows, KEY_VALUE_HEADS * HEAD_WIDTH)
        .astype(jnp.bfloat16)
    )
    head_norm_sums = lax.psum(jnp.stack([grad_query_gain, grad_key_gain]), ("rep", "fsdp"))
    grad_query = rows_product(normalized_rows, d_query)
    grad_key = rows_product(normalized_rows, key_gradient)
    grad_value = rows_product(normalized_rows, value_gradient)
    d_normed = (
        cols_product(d_query, query_full)
        + cols_product(key_gradient, key_full)
        + cols_product(value_gradient, value_full)
    )
    d_input_norm, grad_norm_one = norm_back(d_normed, first_hat, first_scale, norm_one)
    d_tokens = (d_hidden + d_input_norm).astype(jnp.bfloat16)
    attn_shards = (
        lax.psum_scatter(
            grad_query.astype(jnp.bfloat16), "fsdp", scatter_dimension=0, tiled=True
        ).astype(jnp.float32),
        lax.psum_scatter(
            grad_key.astype(jnp.bfloat16), "fsdp", scatter_dimension=0, tiled=True
        ).astype(jnp.float32),
        lax.psum_scatter(
            grad_value.astype(jnp.bfloat16), "fsdp", scatter_dimension=0, tiled=True
        ).astype(jnp.float32),
        lax.psum_scatter(
            grad_out.astype(jnp.bfloat16), "fsdp", scatter_dimension=0, tiled=True
        ).astype(jnp.float32),
        lax.psum_scatter(
            grad_norm_one.astype(jnp.bfloat16), "fsdp", scatter_dimension=0, tiled=True
        ).astype(jnp.float32),
    )
    attn_sums = (
        lax.psum(attn_shards[0].astype(jnp.bfloat16), "rep").astype(jnp.float32),
        lax.psum(attn_shards[1].astype(jnp.bfloat16), "rep").astype(jnp.float32),
        lax.psum(attn_shards[2].astype(jnp.bfloat16), "rep").astype(jnp.float32),
        lax.psum(attn_shards[3].astype(jnp.bfloat16), "rep").astype(jnp.float32),
        lax.psum(attn_shards[4].astype(jnp.bfloat16), "rep").astype(jnp.float32),
    )
    grad_scale = 1.0 / math.sqrt(count_of_rows * rep_count * fsdp_count)
    return (
        mixed,
        d_tokens,
        attn_sums[4] * grad_scale,
        attn_sums[0] * grad_scale,
        attn_sums[1] * grad_scale,
        attn_sums[2] * grad_scale,
        head_norm_sums * grad_scale,
        attn_sums[3] * grad_scale,
        ffn_sums[3] * grad_scale,
        ffn_sums[0] * grad_scale,
        ffn_sums[1] * grad_scale,
        ffn_sums[2] * grad_scale,
    )


def solution(mesh):
    return jax.shard_map(
        per_device,
        mesh=mesh,
        in_specs=(
            P(("rep", "fsdp"), None),
            P(("rep", "fsdp"), None),
            P("fsdp"),
            P("fsdp", None),
            P("fsdp", None),
            P("fsdp", None),
            P(),
            P("fsdp", None),
            P("fsdp"),
            P("fsdp", None),
            P("fsdp", None),
            P("fsdp", None),
            P(("rep", "fsdp"), None),
        ),
        out_specs=(
            P(("rep", "fsdp"), None),
            P(("rep", "fsdp"), None),
            P("fsdp"),
            P("fsdp", None),
            P("fsdp", None),
            P("fsdp", None),
            P(),
            P("fsdp", None),
            P("fsdp"),
            P("fsdp", None),
            P("fsdp", None),
            P("fsdp", None),
        ),
        check_vma=False,
    )
```

profile of v0, /device:TPU:9, one launch (start us, length us, event | category | flops | bytes accessed | tf_op | source)
XLA Modules:
  0.0 1457.7 jit_solution(5098814045108164669)
XLA Ops:
  12.8 6.2 all-gather
  21.2 9.4 all-gather.1
  32.3 22.7 %all-gather.12.cloned.1.call-done = bf16[1024,1024]{1,0:T(8,128)(2,1)} async-done(((bf16[256,1024]{1,0:T(8,128)(2,1)}), bf16[1024,1024]{1,0:T(8,128)(2,1)}) %all-gather.12.cloned.1.call-update) | async-done | bytes 2097168 | tf_op jit(solution)/shard_map/all_gather | solution.py:109
  55.0 2.3 fusion.95
  59.1 42.0 %all-gather.10.cloned.1.call-done = bf16[1024,1024]{1,0:T(8,128)(2,1)} async-done(((bf16[256,1024]{1,0:T(8,128)(2,1)}), bf16[1024,1024]{1,0:T(8,128)(2,1)}) %all-gather.10.cloned.1.call-update) | async-done | bytes 2097168 | tf_op jit(solution)/shard_map/all_gather | solution.py:110
  101.2 2.3 convolution_convert_fusion.9
  106.4 75.2 %all-gather.14.cloned.1.call-done = bf16[1024,2048]{1,0:T(8,128)(2,1)} async-done(((bf16[256,2048]{1,0:T(8,128)(2,1)}), bf16[1024,2048]{1,0:T(8,128)(2,1)}) %all-gather.14.cloned.1.call-update) | async-done | bytes 4194320 | tf_op jit(solution)/shard_map/all_gather | solution.py:108
  181.6 3.5 fusion.93
  190.9 35.4 %while.28 = (s32[]{:T(128)}, bf16[8,256,2,128]{1,3,2,0:T(8,128)(2,1)}, f32[8,2,256]{2,1,0:T(2,128)}, bf16[8,256,128]{1,2,0:T(8,128)(2,1)}, bf16[8,256,128]{2,1,0...) while((s32[]{:T(128)}, ...), condition=%wide.region_9.10_spmd.clone, body=%wide.region_6.9_spmd.clone.sunk | while | flops 68615680 | bytes 2117469 | solution.py:158
  226.3 36.0 %all-gather.16.cloned.1.call-done = bf16[2048,1024]{1,0:T(8,128)(2,1)} async-done(((bf16[512,1024]{1,0:T(8,128)(2,1)}), bf16[2048,1024]{1,0:T(8,128)(2,1)}) %all-gather.16.cloned.1.call-update) | async-done | bytes 4194320 | tf_op jit(solution)/shard_map/all_gather | solution.py:111
  262.3 3.9 multiply_reduce_fusion.6
  267.4 110.0 %all-gather.18.cloned.1.call-done = bf16[1024,3072]{1,0:T(8,128)(2,1)} async-done(((bf16[256,3072]{1,0:T(8,128)(2,1)}), bf16[1024,3072]{1,0:T(8,128)(2,1)}) %all-gather.18.cloned.1.call-update) | async-done | bytes 6291472 | tf_op jit(solution)/shard_map/all_gather | solution.py:162
  377.4 6.2 fusion.100
  383.6 108.8 %all-gather.20.cloned.1.call-done = bf16[1024,3072]{1,0:T(8,128)(2,1)} async-done(((bf16[256,3072]{1,0:T(8,128)(2,1)}), bf16[1024,3072]{1,0:T(8,128)(2,1)}) %all-gather.20.cloned.1.call-update) | async-done | bytes 6291472 | tf_op jit(solution)/shard_map/all_gather | solution.py:163
  492.4 6.2 fusion.101
  498.7 108.9 %all-gather.22.cloned.1.call-done = bf16[3072,1024]{1,0:T(8,128)(2,1)} async-done(((bf16[768,1024]{1,0:T(8,128)(2,1)}), bf16[3072,1024]{1,0:T(8,128)(2,1)}) %all-gather.22.cloned.1.call-update) | async-done | bytes 6291472 | tf_op jit(solution)/shard_map/all_gather | solution.py:164
  607.6 8.8 multiply_convert_fusion.1
  616.5 5.8 fusion.102
  622.5 2.8 multiply_reduce_fusion.3
  626.7 2.3 convolution_convert_fusion.6
  629.0 2.7 reshape.253
  631.7 2.5 copy.171
  634.2 74.3 %while.29 = (s32[]{:T(128)}, f32[8,256,2,128]{1,3,2,0:T(8,128)}, f32[8,256,128]{2,1,0:T(8,128)}, bf16[8,256,128]{1,2,0:T(8,128)(2,1)}, bf16[8,256,128]{2,1,0:T(8...) while((s32[]{:T(128)}, f32[8,256,2,128]{1,3,2,0:T(8,128)}, ...), condition=%wide.region_14.15_spmd.clone, body=%wide.region_12.14_spmd.clone.sunk | while | flops 169442816 | bytes 5325177 | solution.py:247
  719.8 3.2 convolution_convert_fusion.7
  723.8 3.1 fusion.99
  726.9 3.9 copy.126
  730.8 3.7 copy.127
  734.5 2.7 multiply_subtract_fusion
  740.9 3.3 fusion.59
  744.2 3.3 convolution_convert_fusion.5
  748.8 4.6 convolution_convert_fusion.4
  753.4 5.9 convolution_convert_fusion.3
  759.4 5.9 convolution_convert_fusion.2
  766.3 5.9 convolution_convert_fusion.1
  772.3 36.3 %reduce-scatter.12.cloned.1.call-done = bf16[256,1024]{1,0:T(8,128)(2,1)} async-done(((bf16[1024,1024]{1,0:T(8,128)(2,1)}), bf16[256,1024]{1,0:T(8,128)(2,1)}) %reduce-scatter.12.cloned.1.call-update) | async-done | bytes 524304 | tf_op jit(solution)/shard_map/reduce_scatter | solution.py:285
  808.7 80.7 %reduce-scatter.8.cloned.1.call-done = bf16[256,2048]{1,0:T(8,128)(2,1)} async-done(((bf16[1024,2048]{1,0:T(8,128)(2,1)}), bf16[256,2048]{1,0:T(8,128)(2,1)}) %reduce-scatter.8.cloned.1.call-update) | async-done | bytes 1048592 | tf_op jit(solution)/shard_map/reduce_scatter | solution.py:279
  889.4 79.7 %reduce-scatter.14.cloned.1.call-done = bf16[512,1024]{1,0:T(8,128)(2,1)} async-done(((bf16[2048,1024]{1,0:T(8,128)(2,1)}), bf16[512,1024]{1,0:T(8,128)(2,1)}) %reduce-scatter.14.cloned.1.call-update) | async-done | bytes 1048592 | tf_op jit(solution)/shard_map/reduce_scatter | solution.py:288
  969.1 113.4 %reduce-scatter.16.cloned.1.call-done = bf16[256,3072]{1,0:T(8,128)(2,1)} async-done(((bf16[1024,3072]{1,0:T(8,128)(2,1)}), bf16[256,3072]{1,0:T(8,128)(2,1)}) %reduce-scatter.16.cloned.1.call-update) | async-done | bytes 1572880 | tf_op jit(solution)/shard_map/reduce_scatter | solution.py:194
  1082.5 113.6 %reduce-scatter.18.cloned.1.call-done = bf16[256,3072]{1,0:T(8,128)(2,1)} async-done(((bf16[1024,3072]{1,0:T(8,128)(2,1)}), bf16[256,3072]{1,0:T(8,128)(2,1)}) %reduce-scatter.18.cloned.1.call-update) | async-done | bytes 1572880 | tf_op jit(solution)/shard_map/reduce_scatter | solution.py:197
  1196.1 113.5 %reduce-scatter.20.cloned.1.call-done = bf16[768,1024]{1,0:T(8,128)(2,1)} async-done(((bf16[3072,1024]{1,0:T(8,128)(2,1)}), bf16[768,1024]{1,0:T(8,128)(2,1)}) %reduce-scatter.20.cloned.1.call-update) | async-done | bytes 1572880 | tf_op jit(solution)/shard_map/reduce_scatter | solution.py:200
  1311.5 3.6 fusion.103
  1318.8 7.8 all-reduce.4
  1326.8 14.2 all-reduce.2
  1341.1 39.7 %psum.74 = f32[2,128]{1,0:T(2,128)S(1)} all-reduce(f32[2,128]{1,0:T(2,128)S(1)} %pad_maximum_fusion.2), channel_id=1, replica_groups=mesh['rep'=8,'fsdp'=4] {'rep','fsdp'}, use_global_device_ids=true, to_apply=%region_31.32 | all-reduce | flops 256 | bytes 2048 | tf_op jit(solution)/shard_map/psum | solution.py:267
  1383.0 6.0 fusion.65
  1389.0 48.7 %all-reduce.7.cloned.1.call-done = (bf16[256,2048]{1,0:T(8,128)(2,1)}, bf16[256,1024]{1,0:T(8,128)(2,1)}, bf16[256,1024]{1,0:T(8,128)(2,1)}, bf16[512,1024]{1,0:...) async-done(((bf16[256,2048]{1,0:T(8,128)(2,1)}, bf16[256,1024]{1,0:T(8,128)(2,1)}, bf16[256,1024]{1,0:T(8,128)(2,1)}, ...) | async-done | bytes 7864336 | tf_op jit(solution)/shard_map/psum | solution.py:296
  1437.7 3.6 convert_multiply_fusion
  1445.6 3.5 convert_multiply_fusion.1
  (313 shorter events, 162.6 us)
Async XLA Ops:
  7.2 47.8 %all-gather.12.cloned.1.call-start = ((), (), s32[]{:S(2)}) async-start(), calls=%async_computation.8 | async-start | bytes 2621440 | tf_op jit(solution)/shard_map/all_gather | solution.py:109
  7.9 93.3 %all-gather.10.cloned.1.call-start = ((), (), s32[]{:S(2)}) async-start(), calls=%async_computation.7 | async-start | bytes 2621440 | tf_op jit(solution)/shard_map/all_gather | solution.py:110
  8.7 172.9 %all-gather.14.cloned.1.call-start = ((), (), s32[]{:S(2)}) async-start(), calls=%async_computation.9 | async-start | bytes 5242880 | tf_op jit(solution)/shard_map/all_gather | solution.py:108
  9.4 252.9 %all-gather.16.cloned.1.call-start = ((), (), s32[]{:S(2)}) async-start(), calls=%async_computation.10 | async-start | bytes 5242880 | tf_op jit(solution)/shard_map/all_gather | solution.py:111
  10.0 2.8 copy-start.48
  10.0 9.0 copy-start
  10.0 367.4 %all-gather.18.cloned.1.call-start = ((), (), s32[]{:S(2)}) async-start(), calls=%async_computation.11 | async-start | bytes 7864320 | tf_op jit(solution)/shard_map/all_gather | solution.py:162
  10.6 8.6 copy-start.49
  10.6 10.6 copy-start.50
  10.6 481.8 %all-gather.20.cloned.1.call-start = ((), (), s32[]{:S(2)}) async-start(), calls=%async_computation.12 | async-start | bytes 7864320 | tf_op jit(solution)/shard_map/all_gather | solution.py:163
  11.2 596.4 %all-gather.22.cloned.1.call-start = ((), (), s32[]{:S(2)}) async-start(), calls=%async_computation.13 | async-start | bytes 7864320 | tf_op jit(solution)/shard_map/all_gather | solution.py:164
  11.9 760.4 %reduce-scatter.10.cloned.1.call-start = ((), (), s32[]{:S(2)}) async-start(), calls=%async_computation.15 | async-start | bytes 2621440 | tf_op jit(solution)/shard_map/reduce_scatter | solution.py:282
  19.2 82.0 %copy-start.30 = (f32[256]{0:T(256)}, f32[256]{0:T(256)S(1)}, u32[]{:S(2)}) copy-start(f32[256]{0:T(256)S(1)} %add_rsqrt_fusion.3) | copy-start | bytes 3076
  19.8 38.2 %copy-start.42 = (f32[128]{0:T(128)}, f32[128]{0:T(128)S(1)}, u32[]{:S(2)}) copy-start(f32[128]{0:T(128)S(1)} %get-tuple-element.285) | copy-start | bytes 1540
  32.3 73.4 %copy-start.24 = (f32[256,64]{1,0:T(8,128)}, f32[256,64]{1,0:T(8,128)S(1)}, u32[]{:S(2)}) copy-start(f32[256,64]{1,0:T(8,128)S(1)} %get-tuple-element.282) | copy-start | bytes 196612
  226.3 39.9 %copy-start.11 = (bf16[8,256,128]{2,1,0:T(8,128)(2,1)}, bf16[8,256,128]{2,1,0:T(8,128)(2,1)S(1)}, u32[]{:S(2)}) copy-start(bf16[8,256,128]{2,1,0:T(8,128)(2,1)S(1)} %get-tuple-element.527) | copy-start | bytes 1572868
  262.3 4.9 copy-start.34
  616.4 5.8 copy-start.21
  616.4 5.8 copy-start.20
  616.4 5.8 copy-start.14
  616.4 5.8 copy-start.35
  616.4 5.8 copy-start.39
  616.5 6.0 copy-start.45
  622.5 2.8 copy-start.18
  622.5 2.8 copy-start.32
  622.5 4.2 copy-start.46
  712.1 3.4 copy-start.36
  712.9 2.6 copy-start.3
  712.9 2.6 copy-start.12
  715.5 2.1 copy-start.31
  719.8 88.9 %reduce-scatter.12.cloned.1.call-start = ((), (), s32[]{:S(2)}) async-start(), calls=%async_computation.16 | async-start | bytes 2621440 | tf_op jit(solution)/shard_map/reduce_scatter | solution.py:285
  723.1 166.3 %reduce-scatter.8.cloned.1.call-start = ((), (), s32[]{:S(2)}) async-start(), calls=%async_computation.14 | async-start | bytes 5242880 | tf_op jit(solution)/shard_map/reduce_scatter | solution.py:279
  734.5 2.7 copy-start.41
  747.6 221.5 %reduce-scatter.14.cloned.1.call-start = ((), (), s32[]{:S(2)}) async-start(), calls=%async_computation.17 | async-start | bytes 5242880 | tf_op jit(solution)/shard_map/reduce_scatter | solution.py:288
  753.4 329.2 %reduce-scatter.16.cloned.1.call-start = ((), (), s32[]{:S(2)}) async-start(), calls=%async_computation.18 | async-start | bytes 7864320 | tf_op jit(solution)/shard_map/reduce_scatter | solution.py:194
  759.4 436.8 %reduce-scatter.18.cloned.1.call-start = ((), (), s32[]{:S(2)}) async-start(), calls=%async_computation.19 | async-start | bytes 7864320 | tf_op jit(solution)/shard_map/reduce_scatter | solution.py:197
  765.3 544.3 %reduce-scatter.20.cloned.1.call-start = ((), (), s32[]{:S(2)}) async-start(), calls=%async_computation.20 | async-start | bytes 7864320 | tf_op jit(solution)/shard_map/reduce_scatter | solution.py:200
  772.3 665.5 %all-reduce.7.cloned.1.call-start = ((), (), s32[]{:S(2)}) async-start(), calls=%async_computation.21 | async-start | bytes 15728640 | tf_op jit(solution)/shard_map/psum | solution.py:296
  1311.5 3.6 copy-start.6
  1311.5 3.6 copy-start.10
  1316.8 2.1 copy-start.44
  1316.8 24.2 %copy-start.37 = (f32[1024]{0:T(1024)S(1)}, f32[1024]{0:T(1024)}, u32[]{:S(2)}) copy-start(f32[1024]{0:T(1024)} %get-tuple-element.269) | copy-start | bytes 12292
  1380.8 2.2 copy-start.15
  1380.8 2.2 copy-start.16
  1437.7 3.6 copy-start.27
  1442.9 2.6 copy-start.23
  1445.6 3.6 copy-start.28
  1445.6 3.6 copy-start.29
  (19 other events, 24.3 us)
Sparse Core Ops, SparseCore 0:
  9.6 45.3 all-gather.11
  56.6 44.5 all-gather.9
  102.7 78.8 all-gather.13
  183.0 79.2 all-gather.15
  263.8 113.5 all-gather.17
  378.8 113.5 all-gather.19
  494.0 113.5 all-gather.21
  719.9 42.5 reduce-scatter.9
  765.5 43.1 reduce-scatter.11
  810.8 78.5 reduce-scatter.7
  891.8 77.2 reduce-scatter.13
  971.3 111.2 reduce-scatter.15
  1084.8 111.2 reduce-scatter.17
  1198.3 111.2 reduce-scatter.19
  1313.6 124.0 all-reduce.6
where the time goes:
time: 1470 us; the launch traced here: 1460 us
  waiting for transfers between devices  1090 us (74%)
  matrix products  173 us (12%)
  blocking collectives  77.3 us (5%)
  other arithmetic  54.2 us (4%)
  local copies, waits for them, and re-layouts  42 us (3%)
  between operations  15.7 us (1%)
    reduce_scatter x1, waiting for transfers between devices, per_device(): lax.psum_scatter(grad_up.astype(jnp.bfloat16), 'fsdp', scatter_dimension=...  114 us
    reduce_scatter x1, waiting for transfers between devices, per_device(): lax.psum_scatter(grad_down.astype(jnp.bfloat16), 'fsdp', scatter_dimensio...  113 us
    reduce_scatter x1, waiting for transfers between devices, per_device(): lax.psum_scatter(grad_gate.astype(jnp.bfloat16), 'fsdp', scatter_dimensio...  113 us
    all_gather x1, waiting for transfers between devices, per_device(): lax.all_gather(w_gate, 'fsdp', axis=0, tiled=True)  110 us
    all_gather x1, waiting for transfers between devices, per_device(): lax.all_gather(w_down, 'fsdp', axis=0, tiled=True)  109 us
    all_gather x1, waiting for transfers between devices, per_device(): lax.all_gather(w_up, 'fsdp', axis=0, tiled=True)  109 us
    reduce_scatter x1, waiting for transfers between devices, per_device(): lax.psum_scatter(grad_query.astype(jnp.bfloat16), 'fsdp', scatter_dimensi...  80.7 us
    reduce_scatter x1, waiting for transfers between devices, per_device(): lax.psum_scatter(grad_out.astype(jnp.bfloat16), 'fsdp', scatter_dimension...  79.7 us
  transfers between devices with their start and end apart: 15, of which 14 were waited for; matrix products, arithmetic and copies ran while one was open for 10% of the time, Pallas kernels for 0%

commit v1 on v0

v1 whole, which is shorter than its diff:
```python
import functools
import math

import jax
import jax.numpy as jnp
import numpy as np
from jax import lax
from jax.experimental import pallas as pl
from jax.experimental.pallas import tpu as pltpu
from jax.sharding import PartitionSpec as P

EPS = 1e-06
ROPE_BASE = 1000000.0
NEG_FILL = -1e30
HEAD = 128
T = 8
MESH = pl.DeviceIdType.MESH
BF = jnp.bfloat16
F32 = jnp.float32


def mm(a, b):
    return lax.dot_general(a, b, (((1,), (0,)), ((), ())), preferred_element_type=F32)


def mm_nt(a, b):
    return lax.dot_general(a, b, (((1,), (1,)), ((), ())), preferred_element_type=F32)


def mm_tn(a, b):
    return lax.dot_general(a, b, (((0,), (0,)), ((), ())), preferred_element_type=F32)


def rope_table(rows):
    half = HEAD // 2
    freq = np.exp(np.arange(half, dtype=np.float64) * (-2.0 * math.log(ROPE_BASE) / HEAD))
    freq = freq.astype(np.float32)
    angle = (np.arange(rows, dtype=np.float32)[:, None] * freq[None, :]).astype(np.float64)
    cos, sin = np.cos(angle), np.sin(angle)
    full = np.concatenate([cos, cos, -sin, sin], axis=1).astype(np.float32)
    parts = []
    rest = full
    for _ in range(3):
        part = rest.astype(jnp.bfloat16)
        parts.append(part)
        rest = rest - part.astype(np.float32)
    return np.concatenate(parts, axis=1)


def layer_kernel(
    F,
    B,
    D,
    tok_ref,
    cot_ref,
    doc_ref,
    norms_ref,
    hn_ref,
    table_ref,
    wq_ref,
    wk_ref,
    wv_ref,
    wo_ref,
    wg_ref,
    wu_ref,
    wd_ref,
    gqkv_out,
    ggu_out,
    go_out,
    gd_out,
    vec_out,
    mixed_out,
    dtok_out,
    zr_o,
    zr_d,
    ag1,
    ag2,
    ag3,
    ag4,
    st,
    sr,
    rr,
    wqkv,
    wgu,
    wo,
    wd,
    qkpre,
    rot,
    probs,
    att,
    actd,
    hidden,
    dhid,
    normsb,
    zr_gu,
    zr_qkv,
    fq,
    fgu,
    fo,
    fd,
    vz,
    vp,
    ghead,
    ag_s,
    ag_r,
    sib_s,
    sib_r,
    rem_s,
    rem_r,
    w_s,
    w_r,
    nz_s,
    nz_r,
    loc_s,
    zg_s,
    zg_r,
    fin_s,
    fin_r,
    vz_s,
    vz_r,
    vp_s,
    vp_r,
):
    Dz = D // F
    QT = wo.shape[0]
    FT = wd.shape[0]
    GPF = T // F
    half = B // 2
    r = lax.axis_index("rep")
    f = lax.axis_index("fsdp")
    t = lax.rem(r, T)
    base = r - t
    core = lax.rem(t, 2)
    chip = t // 2
    b1 = lax.rem(chip, 2)
    b2 = chip // 2

    def flip(k):
        x = core + (k % 2) * (1 - 2 * core)
        y = b1 + ((k // 2) % 2) * (1 - 2 * b1)
        z = b2 + (k // 4) * (1 - 2 * b2)
        return x + 2 * y + 4 * z

    def unit(rank):
        return lax.rem(rank, 2) * (T // 2) + rank // 2

    g = unit(t)
    fg = g // GPF
    grow = lax.rem(g, GPF)
    sib, xn, yn, dg = base + flip(1), base + flip(2), base + flip(4), base + flip(6)

    def remote(src, dst, ssem, rsem, rep, fs):
        return pltpu.make_async_remote_copy(
            src_ref=src,
            dst_ref=dst,
            send_sem=ssem,
            recv_sem=rsem,
            device_id={"rep": rep, "fsdp": fs},
            device_id_type=MESH,
        )

    def wait_recv(dst, rsem):
        remote(dst, dst, rsem, rsem, sib, f).wait_recv()

    def wait_send(src, ssem):
        remote(src, src, ssem, ssem, sib, f).wait_send()

    barrier = pltpu.get_barrier_semaphore()
    for k in range(1, T):
        pl.semaphore_signal(
            barrier, inc=1, device_id={"rep": base + flip(k), "fsdp": f}, device_id_type=MESH
        )
    for d in range(1, F):
        pl.semaphore_signal(
            barrier, inc=1, device_id={"rep": r, "fsdp": lax.rem(f + d, F)}, device_id_type=MESH
        )

    def own(n):
        return pl.ds(pl.multiple_of(f * n, n), n)

    gq = pl.ds(pl.multiple_of(g * QT, QT), QT)
    gk = pl.ds(pl.multiple_of(g * HEAD, HEAD), HEAD)
    gf = pl.ds(pl.multiple_of(g * FT, HEAD), FT)
    loads = [
        pltpu.make_async_copy(wq_ref.at[:, gq], wqkv.at[own(Dz), pl.ds(0, QT)], loc_s.at[0]),
        pltpu.make_async_copy(wk_ref.at[:, gk], wqkv.at[own(Dz), pl.ds(QT, HEAD)], loc_s.at[1]),
        pltpu.make_async_copy(
            wv_ref.at[:, gk], wqkv.at[own(Dz), pl.ds(QT + HEAD, HEAD)], loc_s.at[2]
        ),
        pltpu.make_async_copy(wg_ref.at[:, gf], wgu.at[own(Dz), pl.ds(0, FT)], loc_s.at[3]),
        pltpu.make_async_copy(wu_ref.at[:, gf], wgu.at[own(Dz), pl.ds(FT, FT)], loc_s.at[4]),
    ]
    for c in loads:
        c.start()

    def row_load(src, dst, rows, sem):
        return pltpu.make_async_copy(
            src.at[pl.ds(pl.multiple_of(grow * rows, rows), rows), :], dst, sem
        )

    @pl.when(f == fg)
    def _():
        row_load(wo_ref, wo, QT, loc_s.at[5]).start()
        row_load(wd_ref, wd, FT, loc_s.at[6]).start()

    normsb[f] = norms_ref[...]
    pl.semaphore_wait(barrier, T - 1 + F - 1)

    def others(fn):
        for d in range(1, F):
            fn(d, lax.rem(f + d, F), lax.rem(f + F - d, F))

    def norms_send(d, to, _):
        remote(normsb.at[f], normsb.at[f], nz_s.at[d], nz_r.at[d], r, to).start()

    others(norms_send)

    def line_copy(item, buf, rows, s, up, m, to):
        part = buf.at[pl.ds(pl.multiple_of(s * rows, rows), rows), :]
        return remote(part, part, w_s.at[item, up, m], w_r.at[item, up, m], r, to)

    def cols_start(item, buf, rows):
        @pl.when(f < F - 1)
        def _():
            line_copy(item, buf, rows, f, 1, 1, f + 1).start()

        @pl.when(f > 0)
        def _():
            line_copy(item, buf, rows, f, 0, 1, f - 1).start()

    def cols_step(item, buf, rows, m):
        @pl.when(f >= m)
        def _():
            line_copy(item, buf, rows, f - m, 1, m, r * 0).wait_recv()
            if m + 1 < F:

                @pl.when(f < F - 1)
                def _():
                    line_copy(item, buf, rows, f - m, 1, m + 1, f + 1).start()

        @pl.when(f + m < F)
        def _():
            line_copy(item, buf, rows, f + m, 0, m, r * 0).wait_recv()
            if m + 1 < F:

                @pl.when(f > 0)
                def _():
                    line_copy(item, buf, rows, f + m, 0, m + 1, f - 1).start()

    def cols_done(item, buf, rows):
        for m in range(1, F):

            @pl.when((f < F - 1) & (f >= m - 1))
            def _():
                line_copy(item, buf, rows, f, 1, m, r * 0).wait_send()

            @pl.when((f > 0) & (f + m - 1 < F))
            def _():
                line_copy(item, buf, rows, f, 0, m, r * 0).wait_send()

    def row_copy(item, buf, up, to):
        return remote(buf, buf, w_s.at[item, up, 0], w_r.at[item, up, 0], r, to)

    def rows_start(item, buf):
        @pl.when((f == fg) & (f < F - 1))
        def _():
            row_copy(item, buf, 1, f + 1).start()

        @pl.when((f == fg) & (f > 0))
        def _():
            row_copy(item, buf, 0, f - 1).start()

    def rows_step(item, buf):
        @pl.when(f > fg)
        def _():
            row_copy(item, buf, 1, r * 0).wait_recv()

            @pl.when(f < F - 1)
            def _():
                row_copy(item, buf, 1, f + 1).start()

        @pl.when(f < fg)
        def _():
            row_copy(item, buf, 0, r * 0).wait_recv()

            @pl.when(f > 0)
            def _():
                row_copy(item, buf, 0, f - 1).start()

    def rows_done(item, buf):
        @pl.when((f >= fg) & (f < F - 1))
        def _():
            row_copy(item, buf, 1, r * 0).wait_send()

        @pl.when((f <= fg) & (f > 0))
        def _():
            row_copy(item, buf, 0, r * 0).wait_send()

    for c in loads[:3]:
        c.wait()
    cols_start(0, wqkv, Dz)

    @pl.when(f == fg)
    def _():
        row_load(wo_ref, wo, QT, loc_s.at[5]).wait()
        row_load(wd_ref, wd, FT, loc_s.at[6]).wait()

    rows_start(1, wo)

    def ag_start(buf, a):
        remote(buf.at[0], buf.at[2], ag_s.at[a, 2], ag_r.at[a, 2], xn, f).start()
        remote(buf.at[0], buf.at[4], ag_s.at[a, 4], ag_r.at[a, 4], yn, f).start()
        remote(buf.at[0], buf.at[1], ag_s.at[a, 1], ag_r.at[a, 1], sib, f).start()

    def ag_cut(buf, slot, lower):
        rows = buf.shape[1]
        return buf.at[slot, pl.ds(half, rows - half), :] if lower else buf.at[slot, pl.ds(0, half), :]

    def ag_pass(buf, a, slot):
        remote(
            buf.at[slot], buf.at[slot + 1], ag_s.at[a, slot + 1], ag_r.at[a, slot + 1], sib, f
        ).start()

    def ag_step(buf, a, i):
        @pl.when(i == 1)
        def _():
            wait_recv(buf.at[1], ag_r.at[a, 1])

        @pl.when(i == 2)
        def _():
            wait_recv(buf.at[2], ag_r.at[a, 2])
            remote(
                ag_cut(buf, 2, 0), ag_cut(buf, 6, 0), ag_s.at[a, 6], ag_r.at[a, 6], yn, f
            ).start()
            ag_pass(buf, a, 2)

        @pl.when(i == 3)
        def _():
            wait_recv(buf.at[4], ag_r.at[a, 4])
            remote(
                ag_cut(buf, 4, 1), ag_cut(buf, 6, 1), ag_s.at[a, 8], ag_r.at[a, 8], xn, f
            ).start()
            ag_pass(buf, a, 4)
            wait_recv(buf.at[3], ag_r.at[a, 3])

        @pl.when(i == 5)
        def _():
            wait_recv(buf.at[5], ag_r.at[a, 5])

        @pl.when(i == 6)
        def _():
            wait_recv(ag_cut(buf, 6, 0), ag_r.at[a, 6])
            wait_recv(ag_cut(buf, 6, 1), ag_r.at[a, 8])
            ag_pass(buf, a, 6)

        @pl.when(i == 7)
        def _():
            wait_recv(buf.at[7], ag_r.at[a, 7])

    def ag_done(buf, a):
        for k in (1, 2, 3, 4, 5, 7):
            wait_send(buf.at[0], ag_s.at[a, k])
        wait_send(ag_cut(buf, 6, 0), ag_s.at[a, 6])
        wait_send(ag_cut(buf, 6, 1), ag_s.at[a, 8])

    def rs_step(buf, q, s, i):
        @pl.when(lax.rem(i, 2) == 1)
        def _():
            remote(
                buf.at[i], sr.at[s, i // 2], sib_s.at[q, i // 2], sib_r.at[q, i // 2], sib, f
            ).start()

        @pl.when((lax.rem(i, 2) == 0) & (i >= 4))
        def _():
            rs_send(buf, q, s, i // 2 - 1)

    def rs_send(buf, q, s, p):
        wait_recv(sr.at[s, p], sib_r.at[q, p])
        buf[2 * p] = (buf[2 * p].astype(F32) + sr[s, p].astype(F32)).astype(BF)
        low = lax.rem(p, 2)
        high = p // 2
        to = r + low * (2 - 4 * b1) + high * (4 - 8 * b2)
        remote(buf.at[2 * p], rr.at[s, p], rem_s.at[q, p], rem_r.at[q, p], to, f).start()

    def rs_total(buf, q, s):
        wait_recv(sr.at[s, 0], sib_r.at[q, 0])
        total = buf[0].astype(F32) + sr[s, 0].astype(F32)
        for p in range(1, 4):
            wait_recv(rr.at[s, p], rem_r.at[q, p])
            total = total + rr[s, p].astype(F32)
        return total

    def rs_done(buf, q):
        for p in range(4):
            wait_send(buf.at[2 * p + 1], sib_s.at[q, p])
            if p > 0:
                wait_send(buf.at[2 * p], rem_s.at[q, p])

    row_ids = lax.broadcasted_iota(jnp.int32, (B, 1), 0)
    lanes_b = lax.broadcasted_iota(jnp.int32, (1, D), 1)
    end = doc_ref[0, 0]
    meta = jnp.where(lanes_b == 0, end, 0)
    slots = doc_ref.shape[1]
    for i in range(1, slots):
        end = end + doc_ref[0, i]
        meta = meta + jnp.where(lanes_b == i, end, 0)
    live = row_ids < end
    tokens = tok_ref[...].astype(F32)
    first_scale = lax.rsqrt(jnp.mean(tokens * tokens, axis=1, keepdims=True) + EPS)

    def norms_wait(d, _, fs):
        wait_recv(normsb.at[fs], nz_r.at[d])

    others(norms_wait)
    gain_one = jnp.concatenate([normsb[j, 0:1, :] for j in range(F)], axis=1)
    gain_two = jnp.concatenate([normsb[j, 1:2, :] for j in range(F)], axis=1)
    ag1[0, 0:B, :] = (tokens * first_scale * gain_one).astype(BF)
    ag1[0, B : B + 16, :] = jnp.broadcast_to(meta.astype(F32), (16, D)).astype(BF)
    ag_start(ag1, 0)
    ag3[0] = jnp.where(live, cot_ref[...].astype(F32), 0.0).astype(BF)
    for m in range(1, F):
        cols_step(0, wqkv, Dz, m)
    rows_step(1, wo)
    for c in loads[3:]:
        c.wait()
    cols_start(2, wgu, Dz)
    rows_start(3, wd)

    gain_q = hn_ref[0:1, :].astype(F32)
    gain_k = hn_ref[1:2, :].astype(F32)
    score_scale = HEAD ** (-0.5)

    def block_layout(i):
        ends = ag1[i, B : B + 16, :][0:1, 0:HEAD].astype(F32)
        rows = lax.broadcasted_iota(jnp.int32, (B, 1), 0).astype(F32)
        cols = lax.broadcasted_iota(jnp.int32, (1, B), 1).astype(F32)
        seg_row = jnp.zeros((B, 1), F32)
        seg_col = jnp.zeros((1, B), F32)
        start = jnp.zeros((B, 1), F32)
        for n in range(slots):
            e = ends[:, n : n + 1]
            past = rows >= e
            seg_row = seg_row + past.astype(F32)
            seg_col = seg_col + (cols >= e).astype(F32)
            start = jnp.maximum(start, jnp.where(past, e, 0.0))
        alive = rows < ends[:, slots - 1 : slots]
        position = rows - jnp.where(alive, start, 0.0)
        return rows, cols, seg_row, seg_col, alive, position

    def rope_rows(position, cols):
        pick = (cols == position).astype(F32).astype(BF)
        table = mm(pick, table_ref[...])
        w = 2 * HEAD
        table = table[:, 0:w] + table[:, w : 2 * w] + table[:, 2 * w : 3 * w]
        return table[:, 0:HEAD], table[:, HEAD:w]

    def rotate(x, cos, sin):
        return x * cos + pltpu.roll(x, HEAD // 2, 1) * sin

    def head_scale(x):
        return lax.rsqrt(jnp.mean(x * x, axis=1, keepdims=True) + EPS)

    def forward_block(i, carry):
        ag_step(ag1, 0, i)

        @pl.when(i == 2)
        def _():
            ag_start(ag3, 2)

        rows, cols, seg_row, seg_col, alive, position = block_layout(i)
        cos, sin = rope_rows(position, cols)
        pre = mm(ag1[i, 0:B, :], wqkv[...])
        qkpre[i] = pre[:, 0 : QT + HEAD]
        parts = []
        for n in range(3):
            x = pre[:, n * HEAD : (n + 1) * HEAD]
            x = x * head_scale(x) * (gain_q if n < 2 else gain_k)
            parts.append(rotate(x, cos, sin).astype(BF))
        v = pre[:, QT + HEAD : QT + 2 * HEAD].astype(BF)
        for n in range(3):
            rot[i, :, n * HEAD : (n + 1) * HEAD] = parts[n]
        rot[i, :, 3 * HEAD : 4 * HEAD] = v
        allowed = ((seg_row == seg_col) & (cols <= rows) & alive) | (cols == rows)
        for n in range(2):
            scores = mm_nt(parts[n], parts[2]) * score_scale
            scores = jnp.where(allowed, scores, NEG_FILL)
            expd = jnp.exp(scores - jnp.max(scores, axis=1, keepdims=True))
            prob = (expd / jnp.sum(expd, axis=1, keepdims=True)).astype(BF)
            probs[i, n * B : (n + 1) * B, :] = prob
            att[i, :, n * HEAD : (n + 1) * HEAD] = mm(prob, v).astype(BF)
        st[i] = mm(att[i], wo[...]).astype(BF)
        rs_step(st, 0, 0, i)
        return carry

    lax.fori_loop(0, T, forward_block, 0)
    rs_send(st, 0, 0, 3)
    cols_step(2, wgu, Dz, 1)
    for i in range(1, T):
        ag_step(ag3, 2, i)
    for m in range(2, F):
        cols_step(2, wgu, Dz, m)
    rows_step(3, wd)
    hid = tokens + rs_total(st, 0, 0)
    rs_done(st, 0)
    hidden[...] = hid
    second_scale = lax.rsqrt(jnp.mean(hid * hid, axis=1, keepdims=True) + EPS)
    ag2[0] = (hid * second_scale * gain_two).astype(BF)
    ag_start(ag2, 1)

    def ffn_block(i, carry):
        ag_step(ag2, 1, i)
        up_gate = mm(ag2[i], wgu[...])
        gate, up = up_gate[:, 0:FT], up_gate[:, FT : 2 * FT]
        sig = 1.0 / (1.0 + jnp.exp(-gate))
        silu = gate * sig
        actd[i, :, 0:FT] = (silu * up).astype(BF)
        d_act = mm_nt(ag3[i], wd[...])
        actd[i, :, FT : 2 * FT] = (d_act * up * sig * (1.0 + gate * (1.0 - sig))).astype(BF)
        actd[i, :, 2 * FT : 3 * FT] = (d_act * silu).astype(BF)
        st[i] = mm_nt(actd[i, :, FT : 3 * FT], wgu[...]).astype(BF)
        rs_step(st, 1, 1, i)
        return carry

    lax.fori_loop(0, T, ffn_block, 0)
    rs_send(st, 1, 1, 3)
    cols_done(2, wgu, Dz)

    step = 256

    def grad_gu(m, carry):
        at = pl.ds(pl.multiple_of(m * step, step), step)
        total = mm_tn(ag2[0, :, at], actd[0, :, FT : 3 * FT])
        for k in range(1, T):
            total = total + mm_tn(ag2[k, :, at], actd[k, :, FT : 3 * FT])
        wgu[at, :] = total.astype(BF)
        return carry

    lax.fori_loop(0, D // step, grad_gu, 0)

    def scatter(item, buf, slots_ref):
        def send(d, to, _):
            remote(
                buf.at[pl.ds(pl.multiple_of(to * Dz, Dz), Dz), :],
                slots_ref.at[f],
                zg_s.at[item, d],
                zg_r.at[item, d],
                r,
                to,
            ).start()

        others(send)

    def scatter_total(item, buf, slots_ref, dst):
        total = buf[own(Dz), :].astype(F32)

        def recv(d, to, fs):
            wait_recv(slots_ref.at[fs], zg_r.at[item, d])

        others(recv)
        for d in range(1, F):
            total = total + slots_ref[lax.rem(f + d, F)].astype(F32)
        dst[...] = total.astype(BF)

    def scatter_done(item, buf):
        for d in range(1, F):
            wait_send(buf.at[own(Dz), :], zg_s.at[item, d])

    scatter(0, wgu, zr_gu)
    d_out = jnp.where(live, cot_ref[...].astype(F32), 0.0)
    pre_two = rs_total(st, 1, 1)
    rs_done(st, 1)
    hid = hidden[...]
    second_scale = lax.rsqrt(jnp.mean(hid * hid, axis=1, keepdims=True) + EPS)
    second_hat = hid * second_scale
    grad_two = jnp.sum(pre_two * second_hat, axis=0, keepdims=True)
    dn_two = pre_two * gain_two
    d_hid = d_out + second_scale * (
        dn_two - second_hat * jnp.mean(dn_two * second_hat, axis=1, keepdims=True)
    )
    dhid[...] = d_hid
    ag4[0] = d_hid.astype(BF)
    ag_start(ag4, 3)

    ag_done(ag2, 1)

    def down_block(i, carry):
        ag2[i] = mm(actd[i, :, 0:FT], wd[...]).astype(BF)

        @pl.when(lax.rem(i, 2) == 1)
        def _():
            remote(
                ag2.at[i], sr.at[0, i // 2], sib_s.at[2, i // 2], sib_r.at[2, i // 2], sib, f
            ).start()

        return carry

    lax.fori_loop(0, T, down_block, 0)
    rows_done(3, wd)

    def grad_down(m, carry):
        at = pl.ds(pl.multiple_of(m * step, step), step)
        total = mm_tn(actd[0, :, 0:FT], ag3[0, :, at])
        for k in range(1, T):
            total = total + mm_tn(actd[k, :, 0:FT], ag3[k, :, at])
        wd[:, at] = total.astype(BF)
        return carry

    lax.fori_loop(0, D // step, grad_down, 0)

    def row_send(item, buf, slots_ref):
        @pl.when(f != fg)
        def _():
            remote(buf, slots_ref.at[f], zg_s.at[item, 0], zg_r.at[item, f], r, fg).start()

    row_send(1, wd, zr_d)
    ag_done(ag3, 2)
    ghead[...] = jnp.zeros_like(ghead)

    def backward_block(i, carry):
        ag_step(ag4, 3, i)
        rows, cols, _, _, _, position = block_layout(i)
        cos, sin = rope_rows(position, cols)
        d_att = mm_nt(ag4[i], wo[...]).astype(BF)
        k_rot = rot[i, :, QT : QT + HEAD]
        v = rot[i, :, QT + HEAD : QT + 2 * HEAD]
        d_v = jnp.zeros((B, HEAD), F32)
        d_k = jnp.zeros((B, HEAD), F32)
        d_pre = []
        sums = []

        def norm_back(grad, n, gain):
            x = qkpre[i, :, n * HEAD : (n + 1) * HEAD]
            scale = head_scale(x)
            hat = x * scale
            dn = rotate(grad, cos, -sin)
            total = jnp.sum(dn * hat, axis=0, keepdims=True)
            dn = dn * gain
            back = scale * (dn - hat * jnp.mean(dn * hat, axis=1, keepdims=True))
            return back.astype(BF), total

        for n in range(2):
            prob = probs[i, n * B : (n + 1) * B, :]
            q_rot = rot[i, :, n * HEAD : (n + 1) * HEAD]
            d_head = d_att[:, n * HEAD : (n + 1) * HEAD]
            d_prob = mm_nt(d_head, v)
            p32 = prob.astype(F32)
            center = jnp.sum(p32 * d_prob, axis=1, keepdims=True)
            d_score = (p32 * (d_prob - center)).astype(BF)
            d_v = d_v + mm_tn(prob, d_head)
            d_k = d_k + mm_tn(d_score, q_rot)
            back, total = norm_back(mm(d_score, k_rot) * score_scale, n, gain_q)
            d_pre.append(back)
            sums.append(total)
        back, total = norm_back(d_k * score_scale, 2, gain_k)
        d_pre.append(back)
        d_pre.append(d_v.astype(BF))
        ghead[0:1, :] += sums[0] + sums[1]
        ghead[1:2, :] += total
        for n in range(4):
            rot[i, :, n * HEAD : (n + 1) * HEAD] = d_pre[n]
        ag3[i] = mm_nt(rot[i], wqkv[...]).astype(BF)
        rs_step(ag3, 3, 1, i)
        return carry

    lax.fori_loop(0, T, backward_block, 0)
    rs_send(ag3, 3, 1, 3)
    for p in range(1, 4):
        rs_send(ag2, 2, 0, p)
    cols_done(0, wqkv, Dz)
    rows_done(1, wo)

    def grad_qkv(m, carry):
        at = pl.ds(pl.multiple_of(m * step, step), step)
        total = mm_tn(ag1[0, 0:B, at], rot[0])
        for k in range(1, T):
            total = total + mm_tn(ag1[k, 0:B, at], rot[k])
        wqkv[at, :] = total.astype(BF)
        return carry

    lax.fori_loop(0, D // step, grad_qkv, 0)
    scatter(3, wqkv, zr_qkv)

    def grad_out(m, carry):
        at = pl.ds(pl.multiple_of(m * step, step), step)
        total = mm_tn(att[0], ag4[0, :, at])
        for k in range(1, T):
            total = total + mm_tn(att[k], ag4[k, :, at])
        wo[:, at] = total.astype(BF)
        return carry

    lax.fori_loop(0, D // step, grad_out, 0)
    row_send(2, wo, zr_o)

    def piece_at(item, out, rows, rank):
        u = unit(rank)
        if item in (0, 3):
            return out.at[u]
        return out.at[pl.ds(pl.multiple_of(lax.rem(u, GPF) * rows, rows), rows), :]

    def fin_start(item, src, out, rows):
        dst = piece_at(item, out, rows, t)
        for k, to in ((2, xn), (4, yn), (6, dg), (1, sib)):
            remote(src, dst, fin_s.at[item, k], fin_r.at[item, k], to, f).start()
        pltpu.make_async_copy(src, dst, fin_s.at[item, 0]).start()

    def fin_wait(item, src, out, rows):
        dst = piece_at(item, out, rows, t)
        for k in (1, 2, 4, 6):
            wait_send(src, fin_s.at[item, k])
        pltpu.make_async_copy(src, dst, fin_s.at[item, 0]).wait()

    def has(item, rank):
        return unit(rank) // GPF == f

    def fin_pass(item, out, rows, k):
        rank = flip(k)
        dst = piece_at(item, out, rows, rank)

        def go():
            wait_recv(dst, fin_r.at[item, k])
            remote(dst, dst, fin_s.at[item, k + 1], fin_r.at[item, k + 1], sib, f).start()

        if item in (0, 3):
            go()
        else:
            pl.when(has(item, rank))(go)

    def fin_end(item, out, rows):
        for k in (1, 3, 5, 7):
            rank = flip(k)
            dst = piece_at(item, out, rows, rank)

            def go():
                wait_recv(dst, fin_r.at[item, k])

            def sent():
                wait_send(dst, fin_s.at[item, k])

            if item in (0, 3):
                go()
                if k > 1:
                    sent()
            else:
                pl.when(has(item, rank))(go)
                if k > 1:
                    pl.when(has(item, flip(k - 1)))(sent)

    scatter_total(0, wgu, zr_gu, fgu)
    fin_start(0, fgu, ggu_out, Dz)

    def row_total(item, buf, slots_ref, dst, rows):
        for d in range(1, F):
            fs = lax.rem(f + d, F)
            wait_recv(slots_ref.at[fs], zg_r.at[item, fs])
        chunk = 128
        for c in range(rows // chunk):
            copies = []
            for d in range(1, F):
                fs = lax.rem(f + d, F)
                copies.append(
                    pltpu.make_async_copy(
                        slots_ref.at[fs, pl.ds(c * chunk, chunk), :],
                        st.at[d, pl.ds(0, chunk), :],
                        loc_s.at[d],
                    )
                )
            for x in copies:
                x.start()
            for x in copies:
                x.wait()
            total = buf[c * chunk : (c + 1) * chunk, :].astype(F32)
            for d in range(1, F):
                total = total + st[d, 0:chunk, :].astype(F32)
            dst[c * chunk : (c + 1) * chunk, :] = total.astype(BF)

    @pl.when(f == fg)
    def _():
        row_total(1, wd, zr_d, fd, FT)
        fin_start(1, fd, gd_out, FT)

    pre_one = rs_total(ag3, 3, 1)
    tokens = tok_ref[...].astype(F32)
    first_scale = lax.rsqrt(jnp.mean(tokens * tokens, axis=1, keepdims=True) + EPS)
    first_hat = tokens * first_scale
    grad_one = jnp.sum(pre_one * first_hat, axis=0, keepdims=True)
    dn_one = pre_one * gain_one
    dtok_out[...] = (
        dhid[...]
        + first_scale
        * (dn_one - first_hat * jnp.mean(dn_one * first_hat, axis=1, keepdims=True))
    ).astype(BF)
    vz[f, 0:1, :] = grad_one
    vz[f, 1:2, :] = grad_two
    vz[f, 2:3, :] = jnp.concatenate(
        [ghead[0:1, :], ghead[1:2, :], jnp.zeros((1, D - 2 * HEAD), F32)], axis=1
    )
    vz[f, 3:8, :] = jnp.zeros((5, D), F32)

    def vec_send(d, to, _):
        remote(vz.at[f], vz.at[f], vz_s.at[d], vz_r.at[d], r, to).start()

    others(vec_send)
    out = hidden[...] + rs_total(ag2, 2, 0)
    mixed_out[...] = jnp.where(live, out, 0.0).astype(BF)

    def vec_recv(d, to, fs):
        wait_recv(vz.at[fs], vz_r.at[d])

    others(vec_recv)
    total = vz[0]
    for j in range(1, F):
        total = total + vz[j]
    vp[t] = total
    for k in range(1, T):
        remote(vp.at[t], vp.at[t], vp_s.at[k], vp_r.at[k], base + flip(k), f).start()

    scatter_total(3, wqkv, zr_qkv, fq)
    fin_start(3, fq, gqkv_out, Dz)

    @pl.when(f == fg)
    def _():
        row_total(2, wo, zr_o, fo, QT)
        fin_start(2, fo, go_out, QT)

    for k in range(1, T):
        wait_recv(vp.at[flip(k)], vp_r.at[k])
    total = vp[0]
    for j in range(1, T):
        total = total + vp[j]
    mine = jnp.zeros((8, Dz), F32)
    for j in range(F):
        mine = mine + jnp.where(f == j, total[:, j * Dz : (j + 1) * Dz], 0.0)
    vec_out[:, 0:Dz] = mine
    vec_out[:, Dz : Dz + 2 * HEAD] = total[:, 0 : 2 * HEAD]

    items = ((0, fgu, ggu_out, Dz), (1, fd, gd_out, FT), (3, fq, gqkv_out, Dz), (2, fo, go_out, QT))
    for k in (2, 4, 6):
        for item, _, dst, rows in items:
            fin_pass(item, dst, rows, k)
    for item, src, dst, rows in items:
        fin_end(item, dst, rows)
        if item in (0, 3):
            fin_wait(item, src, dst, rows)
        else:

            @pl.when(f == fg)
            def _():
                fin_wait(item, src, dst, rows)

    ag_done(ag1, 0)
    ag_done(ag4, 3)
    rs_done(ag2, 2)
    rs_done(ag3, 3)
    scatter_done(0, wgu)
    scatter_done(3, wqkv)

    @pl.when(f != fg)
    def _():
        wait_send(wd, zg_s.at[1, 0])
        wait_send(wo, zg_s.at[2, 0])

    for d in range(1, F):
        wait_send(normsb.at[0], nz_s.at[d])
        wait_send(vz.at[0], vz_s.at[d])
    for k in range(1, T):
        wait_send(vp.at[0], vp_s.at[k])


def finish_kernel(scale, gqkv, ggu, go, gd, oq, ok, ov, og, ou, oo, od):
    x = gqkv[0].astype(F32) * scale
    w = oq.shape[1]
    oq[...] = x[:, 0:w]
    ok[...] = x[:, w : w + HEAD]
    ov[...] = x[:, w + HEAD : w + 2 * HEAD]
    x = ggu[0].astype(F32) * scale
    w = og.shape[1]
    og[...] = x[:, 0:w]
    ou[...] = x[:, w : 2 * w]
    oo[...] = go[...].astype(F32) * scale
    od[...] = gd[...].astype(F32) * scale


def per_device(
    F,
    G,
    tokens,
    doc_lengths,
    attn_norm,
    w_query,
    key_matrix,
    value_matrix,
    head_norms,
    w_out,
    ffn_norm,
    w_gate,
    w_up,
    w_down,
    cotangent,
):
    B, D = tokens.shape
    Dz = D // F
    QW, KW, FF = w_query.shape[1], key_matrix.shape[1], w_gate.shape[1]
    QT, FT = QW // T, FF // T
    QZ, FZ = w_out.shape[0], w_down.shape[0]
    norms = jnp.zeros((8, Dz), F32)
    norms = norms.at[0].set(attn_norm.astype(F32)).at[1].set(ffn_norm.astype(F32))
    table = jnp.asarray(rope_table(B))
    vmem = pl.BlockSpec(memory_space=pltpu.VMEM)
    hbm = pl.BlockSpec(memory_space=pl.ANY)
    dma = pltpu.SemaphoreType.DMA
    sds = jax.ShapeDtypeStruct
    outs = pl.pallas_call(
        functools.partial(layer_kernel, F, B, D),
        out_shape=(
            sds((T, Dz, QT + 2 * HEAD), BF),
            sds((T, Dz, 2 * FT), BF),
            sds((QZ, D), BF),
            sds((FZ, D), BF),
            sds((8, Dz + 2 * HEAD), F32),
            sds((B, D), BF),
            sds((B, D), BF),
            sds((F, QT, D), BF),
            sds((F, FT, D), BF),
        ),
        in_specs=[vmem, vmem, pl.BlockSpec(memory_space=pltpu.SMEM), vmem, vmem, vmem] + [hbm] * 7,
        out_specs=(hbm, hbm, hbm, hbm, vmem, vmem, vmem, hbm, hbm),
        scratch_shapes=[
            pltpu.VMEM((T, B + 16, D), BF),
            pltpu.VMEM((T, B, D), BF),
            pltpu.VMEM((T, B, D), BF),
            pltpu.VMEM((T, B, D), BF),
            pltpu.VMEM((T, B, D), BF),
            pltpu.VMEM((2, 4, B, D), BF),
            pltpu.VMEM((2, 4, B, D), BF),
            pltpu.VMEM((D, QT + 2 * HEAD), BF),
            pltpu.VMEM((D, 2 * FT), BF),
            pltpu.VMEM((QT, D), BF),
            pltpu.VMEM((FT, D), BF),
            pltpu.VMEM((T, B, QT + HEAD), F32),
            pltpu.VMEM((T, B, QT + 2 * HEAD), BF),
            pltpu.VMEM((T, 2 * B, B), BF),
            pltpu.VMEM((T, B, QT), BF),
            pltpu.VMEM((T, B, 3 * FT), BF),
            pltpu.VMEM((B, D), F32),
            pltpu.VMEM((B, D), F32),
            pltpu.VMEM((F, 8, Dz), F32),
            pltpu.VMEM((F, Dz, 2 * FT), BF),
            pltpu.VMEM((F, Dz, QT + 2 * HEAD), BF),
            pltpu.VMEM((Dz, QT + 2 * HEAD), BF),
            pltpu.VMEM((Dz, 2 * FT), BF),
            pltpu.VMEM((QT, D), BF),
            pltpu.VMEM((FT, D), BF),
            pltpu.VMEM((F, 8, D), F32),
            pltpu.VMEM((T, 8, D), F32),
            pltpu.VMEM((8, HEAD), F32),
            dma((4, 9)),
            dma((4, 9)),
            dma((4, 4)),
            dma((4, 4)),
            dma((4, 4)),
            dma((4, 4)),
            dma((4, 2, F)),
            dma((4, 2, F)),
            dma((F,)),
            dma((F,)),
            dma((8,)),
            dma((4, F)),
            dma((4, F)),
            dma((4, T)),
            dma((4, T)),
            dma((F,)),
            dma((F,)),
            dma((T,)),
            dma((T,)),
        ],
        compiler_params=pltpu.CompilerParams(
            collective_id=0, has_side_effects=True, vmem_limit_bytes=62 * 2**20
        ),
    )(
        tokens,
        cotangent,
        doc_lengths,
        norms,
        head_norms,
        table,
        w_query,
        key_matrix,
        value_matrix,
        w_out,
        w_gate,
        w_up,
        w_down,
    )
    gqkv, ggu, go, gd, vec, mixed, d_tokens = outs[:7]
    if G > 1:
        groups = [[t + T * n for n in range(G)] for t in range(T)]
        gqkv, ggu, go, gd = (
            lax.psum(x, "rep", axis_index_groups=groups) for x in (gqkv, ggu, go, gd)
        )
        vec = lax.psum(vec, "rep", axis_index_groups=groups)
    scale = 1.0 / math.sqrt(B * T * G * F)

    def order(u):
        return u

    qb, fb = QZ // T, FZ // T
    oq, ok, ov, og, ou, oo, od = pl.pallas_call(
        functools.partial(finish_kernel, scale),
        grid=(T,),
        out_shape=(
            sds((Dz, QW), F32),
            sds((Dz, KW), F32),
            sds((Dz, KW), F32),
            sds((Dz, FF), F32),
            sds((Dz, FF), F32),
            sds((QZ, D), F32),
            sds((FZ, D), F32),
        ),
        in_specs=[
            pl.BlockSpec((1, Dz, QT + 2 * HEAD), lambda u: (u, 0, 0)),
            pl.BlockSpec((1, Dz, 2 * FT), lambda u: (u, 0, 0)),
            pl.BlockSpec((qb, D), lambda u: (u, 0)),
            pl.BlockSpec((fb, D), lambda u: (u, 0)),
        ],
        out_specs=(
            pl.BlockSpec((Dz, QT), lambda u: (0, u)),
            pl.BlockSpec((Dz, HEAD), lambda u: (0, u)),
            pl.BlockSpec((Dz, HEAD), lambda u: (0, u)),
            pl.BlockSpec((Dz, FT), lambda u: (0, u)),
            pl.BlockSpec((Dz, FT), lambda u: (0, u)),
            pl.BlockSpec((qb, D), lambda u: (u, 0)),
            pl.BlockSpec((fb, D), lambda u: (u, 0)),
        ),
    )(gqkv, ggu, go, gd)
    vec = vec * scale
    return (
        mixed,
        d_tokens,
        vec[0, 0:Dz],
        oq,
        ok,
        ov,
        jnp.concatenate([vec[2:3, Dz : Dz + HEAD], vec[2:3, Dz + HEAD : Dz + 2 * HEAD]], axis=0),
        oo,
        vec[1, 0:Dz],
        og,
        ou,
        od,
    )


def solution(mesh):
    F = mesh.shape["fsdp"]
    G = mesh.shape["rep"] // T
    rows = P(("rep", "fsdp"), None)
    mat = P("fsdp", None)
    vec = P("fsdp")
    return jax.shard_map(
        functools.partial(per_device, F, G),
        mesh=mesh,
        in_specs=(rows, rows, vec, mat, mat, mat, P(), mat, vec, mat, mat, mat, rows),
        out_specs=(rows, rows, vec, mat, mat, mat, P(), mat, vec, mat, mat, mat),
        check_vma=False,
    )
```

time: 1470 us -> 305 us (0.21)
  the two profiles are of different devices: /device:TPU:9 before, /device:TPU:5 now
where the time goes in v1:
time: 305 us; the launch traced here: 304 us
  Pallas kernels  298 us (98%)
  local copies, waits for them, and re-layouts  3.45 us (1%)
    pallas_call x1, Pallas kernels, per_device(): pl.pallas_call(functools.partial(layer_kernel, F, B, D), out_shape=(sds((...  288 us
    pallas_call x1, Pallas kernels, per_device(): pl.pallas_call(functools.partial(finish_kernel, scale), grid=(T,), out_sh...  9.85 us

profile of v1, /device:TPU:5, one launch (start us, length us, event | category | flops | bytes accessed | tf_op | source)
XLA Modules:
  0.0 304.0 jit_solution(5682388349658403690)
XLA Ops:
  0.6 0.7 reshape.78
  1.3 0.7 convert.7
  2.0 0.0 copy-start.2
  2.0 0.6 copy-done.2
  2.6 288.1 %shard_map.229 = (bf16[8,256,512]{2,1,0:T(8,128)(2,1)}, bf16[8,256,768]{2,1,0:T(8,128)(2,1)}, bf16[512,1024]{1,0:T(8,128)(2,1)}, bf16[768,1024]{1,0:T(8,128)(2,1...) custom-call(bf16[256,1024]{1,0:T(8,128)(2,1)} %tok_ref.1, ...), custom_call_target="tpu_custom_call" | custom-call | tf_op jit(solution)/shard_map/pallas_call | solution.py:912
  290.7 0.7 broadcast_multiply_fusion
  291.4 0.6 fusion
  292.0 0.6 pad_maximum_fusion
  292.6 0.0 copy-start.1
  292.6 0.0 copy-start
  292.6 9.8 %shard_map.230 = (f32[256,2048]{1,0:T(8,128)}, f32[256,1024]{1,0:T(8,128)}, f32[256,1024]{1,0:T(8,128)}, f32[256,3072]{1,0:T(8,128)}, f32[256,3072]{1,0:T(8,128)...) custom-call(bf16[8,256,512]{2,1,0:T(8,128)(2,1)} %get-tuple-element.53.gqkv, bf16[8,256,768]{2,1,0:T(8,128)(2,1)} %get-tuple-element.54.ggu, ...), custom_call_target="tpu_custom_call" | custom-call | tf_op jit(solution)/shard_map/pallas_call | solution.py:1007
  302.4 0.0 copy-done.1
  302.4 0.8 copy.29
  303.2 0.0 copy-done
  303.2 0.8 copy.30
  (3 shorter events, 0.0 us)
Async XLA Ops:
  2.0 0.6 copy-start.2
  292.6 9.9 %copy-start.1 = (bf16[256,1024]{1,0:T(8,128)(2,1)S(1)}, bf16[256,1024]{1,0:T(8,128)(2,1)}, u32[]{:S(2)}) copy-start(bf16[256,1024]{1,0:T(8,128)(2,1)} %get-tuple-element.80) | copy-start | bytes 1572868
  292.6 10.7 %copy-start = (bf16[256,1024]{1,0:T(8,128)(2,1)S(1)}, bf16[256,1024]{1,0:T(8,128)(2,1)}, u32[]{:S(2)}) copy-start(bf16[256,1024]{1,0:T(8,128)(2,1)} %get-tuple-element.81) | copy-start | bytes 1572868

commit v2 on v1

--- a/solution.py
+++ b/solution.py
@@ -71,8 +71,6 @@
     vec_out,
     mixed_out,
     dtok_out,
-    zr_o,
-    zr_d,
     ag1,
     ag2,
     ag3,
@@ -93,11 +91,9 @@
     dhid,
     normsb,
     zr_gu,
+    zr_d,
+    zr_o,
     zr_qkv,
-    fq,
-    fgu,
-    fo,
-    fd,
     vz,
     vp,
     ghead,
@@ -270,8 +266,8 @@
         def _():
             row_copy(item, buf, 0, f - 1).start()
 
-    def rows_step(item, buf):
-        @pl.when(f > fg)
+    def rows_step(item, buf, m):
+        @pl.when(f - fg == m)
         def _():
             row_copy(item, buf, 1, r * 0).wait_recv()
 
@@ -279,7 +275,7 @@
             def _():
                 row_copy(item, buf, 1, f + 1).start()
 
-        @pl.when(f < fg)
+        @pl.when(fg - f == m)
         def _():
             row_copy(item, buf, 0, r * 0).wait_recv()
 
@@ -366,9 +362,7 @@
     def rs_step(buf, q, s, i):
         @pl.when(lax.rem(i, 2) == 1)
         def _():
-            remote(
-                buf.at[i], sr.at[s, i // 2], sib_s.at[q, i // 2], sib_r.at[q, i // 2], sib, f
-            ).start()
+            sib_send(buf, q, s, i)
 
         @pl.when((lax.rem(i, 2) == 0) & (i >= 4))
         def _():
@@ -382,10 +376,10 @@
         to = r + low * (2 - 4 * b1) + high * (4 - 8 * b2)
         remote(buf.at[2 * p], rr.at[s, p], rem_s.at[q, p], rem_r.at[q, p], to, f).start()
 
-    def rs_total(buf, q, s):
+    def rs_total(buf, q, s, last=3):
         wait_recv(sr.at[s, 0], sib_r.at[q, 0])
         total = buf[0].astype(F32) + sr[s, 0].astype(F32)
-        for p in range(1, 4):
+        for p in range(1, last + 1):
             wait_recv(rr.at[s, p], rem_r.at[q, p])
             total = total + rr[s, p].astype(F32)
         return total
@@ -395,6 +389,41 @@
             wait_send(buf.at[2 * p + 1], sib_s.at[q, p])
             if p > 0:
                 wait_send(buf.at[2 * p], rem_s.at[q, p])
+
+    upper, lower = pl.ds(0, half), pl.ds(half, half)
+
+    def relay_send(buf, q, s, p):
+        wait_recv(sr.at[s, p], sib_r.at[q, p])
+        at = 2 * p
+        if p == 3:
+            buf[at] = (buf[at].astype(F32) + sr[s, p].astype(F32)).astype(BF)
+            for cut, to, sem in ((upper, xn, 3), (lower, yn, 0)):
+                remote(
+                    buf.at[at, cut, :], rr.at[s, 3, cut, :], rem_s.at[q, sem], rem_r.at[q, sem], to, f
+                ).start()
+            return
+        keep, add, to, sem = (upper, lower, xn, 0) if p == 1 else (lower, upper, yn, 3)
+        wait_recv(rr.at[s, 3, add, :], rem_r.at[q, sem])
+        buf[at, keep, :] = (buf[at, keep, :].astype(F32) + sr[s, p, keep, :].astype(F32)).astype(BF)
+        buf[at, add, :] = (
+            buf[at, add, :].astype(F32)
+            + sr[s, p, add, :].astype(F32)
+            + rr[s, 3, add, :].astype(F32)
+        ).astype(BF)
+        remote(buf.at[at], rr.at[s, p], rem_s.at[q, p], rem_r.at[q, p], to, f).start()
+
+    def relay_done(buf, q):
+        for p in range(4):
+            wait_send(buf.at[2 * p + 1], sib_s.at[q, p])
+        for p in (1, 2):
+            wait_send(buf.at[2 * p], rem_s.at[q, p])
+        wait_send(buf.at[6, upper, :], rem_s.at[q, 3])
+        wait_send(buf.at[6, lower, :], rem_s.at[q, 0])
+
+    def sib_send(buf, q, s, i):
+        remote(
+            buf.at[i], sr.at[s, i // 2], sib_s.at[q, i // 2], sib_r.at[q, i // 2], sib, f
+        ).start()
 
     row_ids = lax.broadcasted_iota(jnp.int32, (B, 1), 0)
     lanes_b = lax.broadcasted_iota(jnp.int32, (1, D), 1)
@@ -418,13 +447,25 @@
     ag1[0, B : B + 16, :] = jnp.broadcast_to(meta.astype(F32), (16, D)).astype(BF)
     ag_start(ag1, 0)
     ag3[0] = jnp.where(live, cot_ref[...].astype(F32), 0.0).astype(BF)
-    for m in range(1, F):
-        cols_step(0, wqkv, Dz, m)
-    rows_step(1, wo)
+
+    def wave(m, first):
+        cols_step(first, (wqkv, None, wgu)[first], Dz, m)
+        rows_step(first + 1, (wo, None, wd)[first], m)
+
+    wave(1, 0)
+    for i in (1, 2, 3):
+        ag_step(ag1, 0, i)
+    for m in range(2, min(F, 3)):
+        wave(m, 0)
+    ag_start(ag3, 2)
+    for m in range(3, F):
+        wave(m, 0)
     for c in loads[3:]:
         c.wait()
     cols_start(2, wgu, Dz)
     rows_start(3, wd)
+    for i in (5, 6, 7):
+        ag_step(ag1, 0, i)
 
     gain_q = hn_ref[0:1, :].astype(F32)
     gain_k = hn_ref[1:2, :].astype(F32)
@@ -460,12 +501,17 @@
     def head_scale(x):
         return lax.rsqrt(jnp.mean(x * x, axis=1, keepdims=True) + EPS)
 
-    def forward_block(i, carry):
-        ag_step(ag1, 0, i)
-
-        @pl.when(i == 2)
-        def _():
-            ag_start(ag3, 2)
+    def forward_block(j, carry):
+        i = lax.rem(j + 6, T)
+
+        @pl.when(j == 3)
+        def _():
+            for n in (1, 2, 3):
+                ag_step(ag3, 2, n)
+
+        @pl.when(j == 4)
+        def _():
+            wave(1, 2)
 
         rows, cols, seg_row, seg_col, alive, position = block_layout(i)
         cos, sin = rope_rows(position, cols)
@@ -489,23 +535,31 @@
             probs[i, n * B : (n + 1) * B, :] = prob
             att[i, :, n * HEAD : (n + 1) * HEAD] = mm(prob, v).astype(BF)
         st[i] = mm(att[i], wo[...]).astype(BF)
-        rs_step(st, 0, 0, i)
+
+        @pl.when(lax.rem(i, 2) == 1)
+        def _():
+            sib_send(st, 0, 0, i)
+
+        for when, p in ((2, 3), (5, 1), (7, 2)):
+
+            @pl.when(j == when)
+            def _():
+                relay_send(st, 0, 0, p)
+
         return carry
 
     lax.fori_loop(0, T, forward_block, 0)
-    rs_send(st, 0, 0, 3)
-    cols_step(2, wgu, Dz, 1)
-    for i in range(1, T):
+    wave(2, 2)
+    for i in (5, 6, 7):
         ag_step(ag3, 2, i)
-    for m in range(2, F):
-        cols_step(2, wgu, Dz, m)
-    rows_step(3, wd)
-    hid = tokens + rs_total(st, 0, 0)
-    rs_done(st, 0)
+    hid = tokens + rs_total(st, 0, 0, 2)
+    relay_done(st, 0)
     hidden[...] = hid
     second_scale = lax.rsqrt(jnp.mean(hid * hid, axis=1, keepdims=True) + EPS)
     ag2[0] = (hid * second_scale * gain_two).astype(BF)
     ag_start(ag2, 1)
+    for m in range(3, F):
+        wave(m, 2)
 
     def ffn_block(i, carry):
         ag_step(ag2, 1, i)
@@ -537,35 +591,115 @@
 
     lax.fori_loop(0, D // step, grad_gu, 0)
 
-    def scatter(item, buf, slots_ref):
-        def send(d, to, _):
-            remote(
-                buf.at[pl.ds(pl.multiple_of(to * Dz, Dz), Dz), :],
-                slots_ref.at[f],
-                zg_s.at[item, d],
-                zg_r.at[item, d],
-                r,
-                to,
-            ).start()
-
-        others(send)
-
-    def scatter_total(item, buf, slots_ref, dst):
-        total = buf[own(Dz), :].astype(F32)
-
-        def recv(d, to, fs):
-            wait_recv(slots_ref.at[fs], zg_r.at[item, d])
-
-        others(recv)
-        for d in range(1, F):
-            total = total + slots_ref[lax.rem(f + d, F)].astype(F32)
-        dst[...] = total.astype(BF)
-
-    def scatter_done(item, buf):
-        for d in range(1, F):
-            wait_send(buf.at[own(Dz), :], zg_s.at[item, d])
-
-    scatter(0, wgu, zr_gu)
+    def hop(item, buf, slots_ref, s, up, to):
+        slot = s if up else s + (F - s) * (1 - (to - s + F - 1) // F)
+        return remote(
+            buf.at[pl.ds(pl.multiple_of(s * Dz, Dz), Dz), :],
+            slots_ref.at[slot],
+            zg_s.at[item, up, s],
+            zg_r.at[item, up, s],
+            r,
+            to,
+        )
+
+    def hop_add(item, buf, slots_ref, s, up, slot):
+        wait_recv(slots_ref.at[slot], zg_r.at[item, up, s])
+        at = pl.ds(pl.multiple_of(s * Dz, Dz), Dz)
+        buf[at, :] = (buf[at, :].astype(F32) + slots_ref[slot].astype(F32)).astype(BF)
+
+    def hops_start(item, buf, slots_ref):
+        @pl.when(f == 0)
+        def _():
+            for s in range(F - 1, 0, -1):
+                hop(item, buf, slots_ref, s, 1, f + 1).start()
+
+        @pl.when(f == F - 1)
+        def _():
+            for s in range(F - 1):
+                hop(item, buf, slots_ref, s, 0, f - 1).start()
+
+    def hops_step(item, buf, slots_ref, n):
+        s = F - n
+
+        @pl.when((f > 0) & (f < s))
+        def _():
+            hop_add(item, buf, slots_ref, s, 1, s)
+            hop(item, buf, slots_ref, s, 1, f + 1).start()
+
+        z = n - 1
+
+        @pl.when((f < F - 1) & (f > z))
+        def _():
+            hop_add(item, buf, slots_ref, z, 0, z)
+            hop(item, buf, slots_ref, z, 0, f - 1).start()
+
+    def hops_total(item, buf, slots_ref):
+        @pl.when(f > 0)
+        def _():
+            hop_add(item, buf, slots_ref, f, 1, f)
+
+        @pl.when(f < F - 1)
+        def _():
+            hop_add(item, buf, slots_ref, f, 0, F)
+
+    def hops_done(item, buf):
+        part = buf.at[pl.ds(0, Dz), :]
+        for s in range(F):
+
+            @pl.when(f < s)
+            def _():
+                wait_send(part, zg_s.at[item, 1, s])
+
+            @pl.when(f > s)
+            def _():
+                wait_send(part, zg_s.at[item, 0, s])
+
+    def row_hop(item, buf, slots_ref, up, to):
+        return remote(buf, slots_ref.at[up], zg_s.at[item, up, 0], zg_r.at[item, up, 0], r, to)
+
+    def row_add(item, buf, slots_ref, up):
+        wait_recv(slots_ref.at[up], zg_r.at[item, up, 0])
+        buf[...] = (buf[...].astype(F32) + slots_ref[up].astype(F32)).astype(BF)
+
+    def row_hops_start(item, buf, slots_ref):
+        @pl.when((f == 0) & (fg > 0))
+        def _():
+            row_hop(item, buf, slots_ref, 1, f + 1).start()
+
+        @pl.when((f == F - 1) & (fg < F - 1))
+        def _():
+            row_hop(item, buf, slots_ref, 0, f - 1).start()
+
+    def row_hops_step(item, buf, slots_ref, n):
+        @pl.when((f < fg) & (f == n))
+        def _():
+            row_add(item, buf, slots_ref, 1)
+            row_hop(item, buf, slots_ref, 1, f + 1).start()
+
+        @pl.when((f > fg) & (F - 1 - f == n))
+        def _():
+            row_add(item, buf, slots_ref, 0)
+            row_hop(item, buf, slots_ref, 0, f - 1).start()
+
+    def row_hops_total(item, buf, slots_ref):
+        @pl.when((f == fg) & (f > 0))
+        def _():
+            row_add(item, buf, slots_ref, 1)
+
+        @pl.when((f == fg) & (f < F - 1))
+        def _():
+            row_add(item, buf, slots_ref, 0)
+
+    def row_hops_done(item, buf):
+        @pl.when(f < fg)
+        def _():
+            wait_send(buf, zg_s.at[item, 1, 0])
+
+        @pl.when(f > fg)
+        def _():
+            wait_send(buf, zg_s.at[item, 0, 0])
+
+    hops_start(0, wgu, zr_gu)
     d_out = jnp.where(live, cot_ref[...].astype(F32), 0.0)
     pre_two = rs_total(st, 1, 1)
     rs_done(st, 1)
@@ -588,9 +722,7 @@
 
         @pl.when(lax.rem(i, 2) == 1)
         def _():
-            remote(
-                ag2.at[i], sr.at[0, i // 2], sib_s.at[2, i // 2], sib_r.at[2, i // 2], sib, f
-            ).start()
+            sib_send(ag2, 2, 0, i)
 
         return carry
 
@@ -607,17 +739,22 @@
 
     lax.fori_loop(0, D // step, grad_down, 0)
 
-    def row_send(item, buf, slots_ref):
-        @pl.when(f != fg)
-        def _():
-            remote(buf, slots_ref.at[f], zg_s.at[item, 0], zg_r.at[item, f], r, fg).start()
-
-    row_send(1, wd, zr_d)
+    row_hops_start(1, wd, zr_d)
     ag_done(ag3, 2)
     ghead[...] = jnp.zeros_like(ghead)
 
     def backward_block(i, carry):
         ag_step(ag4, 3, i)
+        for n in range(1, min(F, 4)):
+
+            @pl.when(i == 2 * n)
+            def _():
+                hops_step(0, wgu, zr_gu, n)
+
+            @pl.when(i == 2 * n + 1)
+            def _():
+                row_hops_step(1, wd, zr_d, n)
+
         rows, cols, _, _, _, position = block_layout(i)
         cos, sin = rope_rows(position, cols)
         d_att = mm_nt(ag4[i], wo[...]).astype(BF)
@@ -660,14 +797,32 @@
             rot[i, :, n * HEAD : (n + 1) * HEAD] = d_pre[n]
         ag3[i] = mm_nt(rot[i], wqkv[...]).astype(BF)
         rs_step(ag3, 3, 1, i)
+        for when, p in ((4, 3), (6, 1), (7, 2)):
+
+            @pl.when(i == when)
+            def _():
+                relay_send(ag2, 2, 0, p)
+
         return carry
 
     lax.fori_loop(0, T, backward_block, 0)
     rs_send(ag3, 3, 1, 3)
-    for p in range(1, 4):
-        rs_send(ag2, 2, 0, p)
+    for n in range(4, F):
+        hops_step(0, wgu, zr_gu, n)
+        row_hops_step(1, wd, zr_d, n)
     cols_done(0, wqkv, Dz)
     rows_done(1, wo)
+
+    def grad_out(m, carry):
+        at = pl.ds(pl.multiple_of(m * step, step), step)
+        total = mm_tn(att[0], ag4[0, :, at])
+        for k in range(1, T):
+            total = total + mm_tn(att[k], ag4[k, :, at])
+        wo[:, at] = total.astype(BF)
+        return carry
+
+    lax.fori_loop(0, D // step, grad_out, 0)
+    row_hops_start(2, wo, zr_o)
 
     def grad_qkv(m, carry):
         at = pl.ds(pl.multiple_of(m * step, step), step)
@@ -678,105 +833,80 @@
         return carry
 
     lax.fori_loop(0, D // step, grad_qkv, 0)
-    scatter(3, wqkv, zr_qkv)
-
-    def grad_out(m, carry):
-        at = pl.ds(pl.multiple_of(m * step, step), step)
-        total = mm_tn(att[0], ag4[0, :, at])
-        for k in range(1, T):
-            total = total + mm_tn(att[k], ag4[k, :, at])
-        wo[:, at] = total.astype(BF)
-        return carry
-
-    lax.fori_loop(0, D // step, grad_out, 0)
-    row_send(2, wo, zr_o)
-
-    def piece_at(item, out, rows, rank):
+    hops_start(3, wqkv, zr_qkv)
+
+    def piece_at(item, out, rows, rank, cut=None):
         u = unit(rank)
+        start, size = (0, rows) if cut is None else (cut * (rows // 2), rows // 2)
         if item in (0, 3):
-            return out.at[u]
-        return out.at[pl.ds(pl.multiple_of(lax.rem(u, GPF) * rows, rows), rows), :]
+            return out.at[u, pl.ds(start, size), :]
+        first = pl.multiple_of(lax.rem(u, GPF) * rows + start, rows // 2)
+        return out.at[pl.ds(first, size), :]
+
+    def has(item, rank, fn):
+        if item in (0, 3):
+            fn()
+        else:
+            pl.when(unit(rank) // GPF == f)(fn)
+
+    def fin_copy(item, src, dst, sem, to):
+        return remote(src, dst, fin_s.at[item, sem], fin_r.at[item, sem], to, f)
 
     def fin_start(item, src, out, rows):
-        dst = piece_at(item, out, rows, t)
-        for k, to in ((2, xn), (4, yn), (6, dg), (1, sib)):
-            remote(src, dst, fin_s.at[item, k], fin_r.at[item, k], to, f).start()
-        pltpu.make_async_copy(src, dst, fin_s.at[item, 0]).start()
-
-    def fin_wait(item, src, out, rows):
-        dst = piece_at(item, out, rows, t)
-        for k in (1, 2, 4, 6):
-            wait_send(src, fin_s.at[item, k])
-        pltpu.make_async_copy(src, dst, fin_s.at[item, 0]).wait()
-
-    def has(item, rank):
-        return unit(rank) // GPF == f
-
-    def fin_pass(item, out, rows, k):
+        def go():
+            dst = piece_at(item, out, rows, t)
+            fin_copy(item, src, dst, 2, xn).start()
+            fin_copy(item, src, dst, 4, yn).start()
+            fin_copy(item, src, dst, 1, sib).start()
+            pltpu.make_async_copy(src, dst, fin_s.at[item, 0]).start()
+
+        has(item, t, go)
+
+    def fin_step(item, out, rows, k):
         rank = flip(k)
-        dst = piece_at(item, out, rows, rank)
+        full = piece_at(item, out, rows, rank)
 
         def go():
-            wait_recv(dst, fin_r.at[item, k])
-            remote(dst, dst, fin_s.at[item, k + 1], fin_r.at[item, k + 1], sib, f).start()
-
-        if item in (0, 3):
-            go()
-        else:
-            pl.when(has(item, rank))(go)
-
-    def fin_end(item, out, rows):
+            if k < 6:
+                wait_recv(full, fin_r.at[item, k])
+                part = piece_at(item, out, rows, rank, k // 4)
+                fin_copy(item, part, part, 4 + k, yn if k == 2 else xn).start()
+            else:
+                wait_recv(piece_at(item, out, rows, rank, 0), fin_r.at[item, 6])
+                wait_recv(piece_at(item, out, rows, rank, 1), fin_r.at[item, 8])
+            fin_copy(item, full, full, k + 1, sib).start()
+
+        has(item, rank, go)
+
+    def fin_end(item, src, out, rows):
         for k in (1, 3, 5, 7):
-            rank = flip(k)
-            dst = piece_at(item, out, rows, rank)
-
-            def go():
-                wait_recv(dst, fin_r.at[item, k])
-
-            def sent():
-                wait_send(dst, fin_s.at[item, k])
-
-            if item in (0, 3):
-                go()
-                if k > 1:
-                    sent()
-            else:
-                pl.when(has(item, rank))(go)
-                if k > 1:
-                    pl.when(has(item, flip(k - 1)))(sent)
-
-    scatter_total(0, wgu, zr_gu, fgu)
-    fin_start(0, fgu, ggu_out, Dz)
-
-    def row_total(item, buf, slots_ref, dst, rows):
-        for d in range(1, F):
-            fs = lax.rem(f + d, F)
-            wait_recv(slots_ref.at[fs], zg_r.at[item, fs])
-        chunk = 128
-        for c in range(rows // chunk):
-            copies = []
-            for d in range(1, F):
-                fs = lax.rem(f + d, F)
-                copies.append(
-                    pltpu.make_async_copy(
-                        slots_ref.at[fs, pl.ds(c * chunk, chunk), :],
-                        st.at[d, pl.ds(0, chunk), :],
-                        loc_s.at[d],
-                    )
-                )
-            for x in copies:
-                x.start()
-            for x in copies:
-                x.wait()
-            total = buf[c * chunk : (c + 1) * chunk, :].astype(F32)
-            for d in range(1, F):
-                total = total + st[d, 0:chunk, :].astype(F32)
-            dst[c * chunk : (c + 1) * chunk, :] = total.astype(BF)
-
-    @pl.when(f == fg)
-    def _():
-        row_total(1, wd, zr_d, fd, FT)
-        fin_start(1, fd, gd_out, FT)
+            full = piece_at(item, out, rows, flip(k))
+            has(item, flip(k), lambda: wait_recv(full, fin_r.at[item, k]))
+
+        def mine():
+            for k in (1, 2, 4):
+                wait_send(src, fin_s.at[item, k])
+            pltpu.make_async_copy(src, piece_at(item, out, rows, t), fin_s.at[item, 0]).wait()
+
+        has(item, t, mine)
+        for k in (2, 4, 6):
+            full = piece_at(item, out, rows, flip(k))
+            part = piece_at(item, out, rows, flip(k), 0)
+
+            def passed():
+                wait_send(full, fin_s.at[item, k + 1])
+                if k < 6:
+                    wait_send(part, fin_s.at[item, 4 + k])
+
+            has(item, flip(k), passed)
+
+    gu_piece, qkv_piece = wgu.at[own(Dz), :], wqkv.at[own(Dz), :]
+    hops_total(0, wgu, zr_gu)
+    fin_start(0, gu_piece, ggu_out, Dz)
+    row_hops_total(1, wd, zr_d)
+    fin_start(1, wd, gd_out, FT)
+    hops_step(3, wqkv, zr_qkv, 1)
+    row_hops_step(2, wo, zr_o, 1)
 
     pre_one = rs_total(ag3, 3, 1)
     tokens = tok_ref[...].astype(F32)
@@ -800,8 +930,19 @@
         remote(vz.at[f], vz.at[f], vz_s.at[d], vz_r.at[d], r, to).start()
 
     others(vec_send)
-    out = hidden[...] + rs_total(ag2, 2, 0)
-    mixed_out[...] = jnp.where(live, out, 0.0).astype(BF)
+    for n in range(2, F):
+        hops_step(3, wqkv, zr_qkv, n)
+        row_hops_step(2, wo, zr_o, n)
+        if n == 2:
+            for k in (2, 4):
+                fin_step(0, ggu_out, Dz, k)
+                fin_step(1, gd_out, FT, k)
+            out = hidden[...] + rs_total(ag2, 2, 0, 2)
+            mixed_out[...] = jnp.where(live, out, 0.0).astype(BF)
+    hops_total(3, wqkv, zr_qkv)
+    fin_start(3, qkv_piece, gqkv_out, Dz)
+    row_hops_total(2, wo, zr_o)
+    fin_start(2, wo, go_out, QT)
 
     def vec_recv(d, to, fs):
         wait_recv(vz.at[fs], vz_r.at[d])
@@ -813,15 +954,8 @@
     vp[t] = total
     for k in range(1, T):
         remote(vp.at[t], vp.at[t], vp_s.at[k], vp_r.at[k], base + flip(k), f).start()
-
-    scatter_total(3, wqkv, zr_qkv, fq)
-    fin_start(3, fq, gqkv_out, Dz)
-
-    @pl.when(f == fg)
-    def _():
-        row_total(2, wo, zr_o, fo, QT)
-        fin_start(2, fo, go_out, QT)
-
+    fin_step(0, ggu_out, Dz, 6)
+    fin_step(1, gd_out, FT, 6)
     for k in range(1, T):
         wait_recv(vp.at[flip(k)], vp_r.at[k])
     total = vp[0]
@@ -832,33 +966,22 @@
         mine = mine + jnp.where(f == j, total[:, j * Dz : (j + 1) * Dz], 0.0)
     vec_out[:, 0:Dz] = mine
     vec_out[:, Dz : Dz + 2 * HEAD] = total[:, 0 : 2 * HEAD]
-
-    items = ((0, fgu, ggu_out, Dz), (1, fd, gd_out, FT), (3, fq, gqkv_out, Dz), (2, fo, go_out, QT))
     for k in (2, 4, 6):
-        for item, _, dst, rows in items:
-            fin_pass(item, dst, rows, k)
-    for item, src, dst, rows in items:
-        fin_end(item, dst, rows)
-        if item in (0, 3):
-            fin_wait(item, src, dst, rows)
-        else:
-
-            @pl.when(f == fg)
-            def _():
-                fin_wait(item, src, dst, rows)
+        fin_step(3, gqkv_out, Dz, k)
+        fin_step(2, go_out, QT, k)
+    fin_end(0, gu_piece, ggu_out, Dz)
+    fin_end(1, wd, gd_out, FT)
+    fin_end(3, qkv_piece, gqkv_out, Dz)
+    fin_end(2, wo, go_out, QT)
 
     ag_done(ag1, 0)
     ag_done(ag4, 3)
-    rs_done(ag2, 2)
+    relay_done(ag2, 2)
     rs_done(ag3, 3)
-    scatter_done(0, wgu)
-    scatter_done(3, wqkv)
-
-    @pl.when(f != fg)
-    def _():
-        wait_send(wd, zg_s.at[1, 0])
-        wait_send(wo, zg_s.at[2, 0])
-
+    hops_done(0, wgu)
+    hops_done(3, wqkv)
+    row_hops_done(1, wd)
+    row_hops_done(2, wo)
     for d in range(1, F):
         wait_send(normsb.at[0], nz_s.at[d])
         wait_send(vz.at[0], vz_s.at[d])
@@ -919,11 +1042,9 @@
             sds((8, Dz + 2 * HEAD), F32),
             sds((B, D), BF),
             sds((B, D), BF),
-            sds((F, QT, D), BF),
-            sds((F, FT, D), BF),
         ),
         in_specs=[vmem, vmem, pl.BlockSpec(memory_space=pltpu.SMEM), vmem, vmem, vmem] + [hbm] * 7,
-        out_specs=(hbm, hbm, hbm, hbm, vmem, vmem, vmem, hbm, hbm),
+        out_specs=(hbm, hbm, hbm, hbm, vmem, vmem, vmem),
         scratch_shapes=[
             pltpu.VMEM((T, B + 16, D), BF),
             pltpu.VMEM((T, B, D), BF),
@@ -944,12 +1065,10 @@
             pltpu.VMEM((B, D), F32),
             pltpu.VMEM((B, D), F32),
             pltpu.VMEM((F, 8, Dz), F32),
-            pltpu.VMEM((F, Dz, 2 * FT), BF),
-            pltpu.VMEM((F, Dz, QT + 2 * HEAD), BF),
-            pltpu.VMEM((Dz, QT + 2 * HEAD), BF),
-            pltpu.VMEM((Dz, 2 * FT), BF),
-            pltpu.VMEM((QT, D), BF),
-            pltpu.VMEM((FT, D), BF),
+            pltpu.VMEM((F + 1, Dz, 2 * FT), BF),
+            pltpu.VMEM((2, FT, D), BF),
+            pltpu.VMEM((2, QT, D), BF),
+            pltpu.VMEM((F + 1, Dz, QT + 2 * HEAD), BF),
             pltpu.VMEM((F, 8, D), F32),
             pltpu.VMEM((T, 8, D), F32),
             pltpu.VMEM((8, HEAD), F32),
@@ -964,10 +1083,10 @@
             dma((F,)),
             dma((F,)),
             dma((8,)),
-            dma((4, F)),
-            dma((4, F)),
-            dma((4, T)),
-            dma((4, T)),
+            dma((4, 2, F)),
+            dma((4, 2, F)),
+            dma((4, 9)),
+            dma((4, 9)),
             dma((F,)),
             dma((F,)),
             dma((T,)),
@@ -991,7 +1110,7 @@
         w_up,
         w_down,
     )
-    gqkv, ggu, go, gd, vec, mixed, d_tokens = outs[:7]
+    gqkv, ggu, go, gd, vec, mixed, d_tokens = outs
     if G > 1:
         groups = [[t + T * n for n in range(G)] for t in range(T)]
         gqkv, ggu, go, gd = (

time: 305 us -> 279 us (0.915)
  the two profiles are of different devices: /device:TPU:5 before, /device:TPU:9 now
where the time goes in v2:
time: 279 us
  Pallas kernels  272 us (97%)
  local copies, waits for them, and re-layouts  3.45 us (1%)
    pallas_call x1, Pallas kernels, per_device(): pl.pallas_call(functools.partial(layer_kernel, F, B, D), out_shape=(sds((...  263 us
    pallas_call x1, Pallas kernels, per_device(): pl.pallas_call(functools.partial(finish_kernel, scale), grid=(T,), out_sh...  9.85 us

profile of v2, /device:TPU:9, one launch (start us, length us, event | category | flops | bytes accessed | tf_op | source)
XLA Modules:
  0.0 278.6 jit_solution(3347736326153958659)
XLA Ops:
  0.6 0.7 reshape.78
  1.3 0.7 convert.7
  2.0 0.0 copy-start.2
  2.0 0.6 copy-done.2
  2.6 262.6 %shard_map.229 = (bf16[8,256,512]{2,1,0:T(8,128)(2,1)}, bf16[8,256,768]{2,1,0:T(8,128)(2,1)}, bf16[512,1024]{1,0:T(8,128)(2,1)}, bf16[768,1024]{1,0:T(8,128)(2,1...) custom-call(bf16[256,1024]{1,0:T(8,128)(2,1)} %tok_ref.1, bf16[256,1024]{1,0:T(8,128)(2,1)} %cot_ref.1, ...), custom_call_target="tpu_custom_call" | custom-call | tf_op jit(solution)/shard_map/pallas_call | solution.py:1035
  265.2 0.7 broadcast_multiply_fusion
  266.0 0.6 fusion
  266.5 0.6 pad_maximum_fusion
  267.1 0.0 copy-start.1
  267.1 0.0 copy-start
  267.1 9.8 %shard_map.230 = (f32[256,2048]{1,0:T(8,128)}, f32[256,1024]{1,0:T(8,128)}, f32[256,1024]{1,0:T(8,128)}, f32[256,3072]{1,0:T(8,128)}, f32[256,3072]{1,0:T(8,128)...) custom-call(bf16[8,256,512]{2,1,0:T(8,128)(2,1)} %get-tuple-element.53.gqkv, bf16[8,256,768]{2,1,0:T(8,128)(2,1)} %get-tuple-element.54.ggu, ...), custom_call_target="tpu_custom_call" | custom-call | tf_op jit(solution)/shard_map/pallas_call | solution.py:1126
  277.0 0.0 copy-done.1
  277.0 0.8 copy.29
  277.8 0.0 copy-done
  277.8 0.8 copy.30
  (3 shorter events, 0.0 us)
Async XLA Ops:
  2.0 0.6 copy-start.2
  267.1 9.9 %copy-start.1 = (bf16[256,1024]{1,0:T(8,128)(2,1)S(1)}, bf16[256,1024]{1,0:T(8,128)(2,1)}, u32[]{:S(2)}) copy-start(bf16[256,1024]{1,0:T(8,128)(2,1)} %get-tuple-element.80) | copy-start | bytes 1572868
  267.1 10.7 %copy-start = (bf16[256,1024]{1,0:T(8,128)(2,1)S(1)}, bf16[256,1024]{1,0:T(8,128)(2,1)}, u32[]{:S(2)}) copy-start(bf16[256,1024]{1,0:T(8,128)(2,1)} %get-tuple-element.81) | copy-start | bytes 1572868

commit v3 on v2

--- a/solution.py
+++ b/solution.py
@@ -37,7 +37,7 @@
     freq = freq.astype(np.float32)
     angle = (np.arange(rows, dtype=np.float32)[:, None] * freq[None, :]).astype(np.float64)
     cos, sin = np.cos(angle), np.sin(angle)
-    full = np.concatenate([cos, cos, -sin, sin], axis=1).astype(np.float32)
+    full = np.concatenate([cos, sin], axis=1).astype(np.float32)
     parts = []
     rest = full
     for _ in range(3):
@@ -97,6 +97,7 @@
     vz,
     vp,
     ghead,
+    turn,
     ag_s,
     ag_r,
     sib_s,
@@ -374,14 +375,14 @@
         low = lax.rem(p, 2)
         high = p // 2
         to = r + low * (2 - 4 * b1) + high * (4 - 8 * b2)
-        remote(buf.at[2 * p], rr.at[s, p], rem_s.at[q, p], rem_r.at[q, p], to, f).start()
-
-    def rs_total(buf, q, s, last=3):
+        remote(buf.at[2 * p], rr.at[s, p - 1], rem_s.at[q, p], rem_r.at[q, p], to, f).start()
+
+    def rs_total(buf, q, s):
         wait_recv(sr.at[s, 0], sib_r.at[q, 0])
         total = buf[0].astype(F32) + sr[s, 0].astype(F32)
-        for p in range(1, last + 1):
-            wait_recv(rr.at[s, p], rem_r.at[q, p])
-            total = total + rr[s, p].astype(F32)
+        for p in range(1, 4):
+            wait_recv(rr.at[s, p - 1], rem_r.at[q, p])
+            total = total + rr[s, p - 1].astype(F32)
         return total
 
     def rs_done(buf, q):
@@ -392,33 +393,47 @@
 
     upper, lower = pl.ds(0, half), pl.ds(half, half)
 
-    def relay_send(buf, q, s, p):
-        wait_recv(sr.at[s, p], sib_r.at[q, p])
+    def relay_send(buf, q, s, p, own):
         at = 2 * p
         if p == 3:
+            wait_recv(sr.at[s, p], sib_r.at[q, p])
             buf[at] = (buf[at].astype(F32) + sr[s, p].astype(F32)).astype(BF)
             for cut, to, sem in ((upper, xn, 3), (lower, yn, 0)):
                 remote(
-                    buf.at[at, cut, :], rr.at[s, 3, cut, :], rem_s.at[q, sem], rem_r.at[q, sem], to, f
+                    buf.at[at, cut, :], rr.at[s, 2, cut, :], rem_s.at[q, sem], rem_r.at[q, sem], to, f
                 ).start()
             return
         keep, add, to, sem = (upper, lower, xn, 0) if p == 1 else (lower, upper, yn, 3)
-        wait_recv(rr.at[s, 3, add, :], rem_r.at[q, sem])
-        buf[at, keep, :] = (buf[at, keep, :].astype(F32) + sr[s, p, keep, :].astype(F32)).astype(BF)
-        buf[at, add, :] = (
-            buf[at, add, :].astype(F32)
-            + sr[s, p, add, :].astype(F32)
-            + rr[s, 3, add, :].astype(F32)
-        ).astype(BF)
-        remote(buf.at[at], rr.at[s, p], rem_s.at[q, p], rem_r.at[q, p], to, f).start()
+        cut = keep if own else add
+        if own:
+            wait_recv(sr.at[s, p], sib_r.at[q, p])
+        else:
+            wait_recv(rr.at[s, 2, add, :], rem_r.at[q, sem])
+        total = buf[at, cut, :].astype(F32) + sr[s, p, cut, :].astype(F32)
+        if not own:
+            total = total + rr[s, 2, add, :].astype(F32)
+        buf[at, cut, :] = total.astype(BF)
+        sem = p if own else p + 3
+        remote(
+            buf.at[at, cut, :], rr.at[s, p - 1, cut, :], rem_s.at[q, sem], rem_r.at[q, sem], to, f
+        ).start()
+
+    def relay_total(buf, q, s):
+        wait_recv(sr.at[s, 0], sib_r.at[q, 0])
+        for sem in (1, 2, 4, 5):
+            wait_recv(rr.at[s, 0, upper, :], rem_r.at[q, sem])
+        return (
+            buf[0].astype(F32)
+            + sr[s, 0].astype(F32)
+            + rr[s, 0].astype(F32)
+            + rr[s, 1].astype(F32)
+        )
 
     def relay_done(buf, q):
         for p in range(4):
             wait_send(buf.at[2 * p + 1], sib_s.at[q, p])
-        for p in (1, 2):
-            wait_send(buf.at[2 * p], rem_s.at[q, p])
-        wait_send(buf.at[6, upper, :], rem_s.at[q, 3])
-        wait_send(buf.at[6, lower, :], rem_s.at[q, 0])
+        for sem in range(6):
+            wait_send(buf.at[6, upper, :], rem_s.at[q, sem])
 
     def sib_send(buf, q, s, i):
         remote(
@@ -447,25 +462,6 @@
     ag1[0, B : B + 16, :] = jnp.broadcast_to(meta.astype(F32), (16, D)).astype(BF)
     ag_start(ag1, 0)
     ag3[0] = jnp.where(live, cot_ref[...].astype(F32), 0.0).astype(BF)
-
-    def wave(m, first):
-        cols_step(first, (wqkv, None, wgu)[first], Dz, m)
-        rows_step(first + 1, (wo, None, wd)[first], m)
-
-    wave(1, 0)
-    for i in (1, 2, 3):
-        ag_step(ag1, 0, i)
-    for m in range(2, min(F, 3)):
-        wave(m, 0)
-    ag_start(ag3, 2)
-    for m in range(3, F):
-        wave(m, 0)
-    for c in loads[3:]:
-        c.wait()
-    cols_start(2, wgu, Dz)
-    rows_start(3, wd)
-    for i in (5, 6, 7):
-        ag_step(ag1, 0, i)
 
     gain_q = hn_ref[0:1, :].astype(F32)
     gain_k = hn_ref[1:2, :].astype(F32)
@@ -491,9 +487,13 @@
     def rope_rows(position, cols):
         pick = (cols == position).astype(F32).astype(BF)
         table = mm(pick, table_ref[...])
-        w = 2 * HEAD
-        table = table[:, 0:w] + table[:, w : 2 * w] + table[:, 2 * w : 3 * w]
-        return table[:, 0:HEAD], table[:, HEAD:w]
+        return table[:, 0:HEAD] + table[:, HEAD : 2 * HEAD] + table[:, 2 * HEAD : 3 * HEAD]
+
+    def turns(i):
+        x = turn[i]
+        y = pltpu.roll(x, HEAD // 2, 1)
+        first = lax.broadcasted_iota(jnp.int32, x.shape, 1) < HEAD // 2
+        return jnp.where(first, x, y), jnp.where(first, -y, x)
 
     def rotate(x, cos, sin):
         return x * cos + pltpu.roll(x, HEAD // 2, 1) * sin
@@ -501,8 +501,38 @@
     def head_scale(x):
         return lax.rsqrt(jnp.mean(x * x, axis=1, keepdims=True) + EPS)
 
+    def prepare(i, carry):
+        rows, cols, seg_row, seg_col, alive, position = block_layout(i)
+        turn[i] = rope_rows(position, cols)
+        allowed = ((seg_row == seg_col) & (cols <= rows) & alive) | (cols == rows)
+        ag4[i, :, 0:B] = jnp.where(allowed, 0.0, NEG_FILL).astype(BF)
+        return carry
+
+    def wave(m, first):
+        cols_step(first, (wqkv, None, wgu)[first], Dz, m)
+        rows_step(first + 1, (wo, None, wd)[first], m)
+
+    wave(1, 0)
+    for i in (1, 2, 3):
+        ag_step(ag1, 0, i)
+    for m in range(2, min(F, 3)):
+        wave(m, 0)
+    ag_start(ag3, 2)
+    lax.fori_loop(0, 5, prepare, 0)
+    for m in range(3, F):
+        wave(m, 0)
+    for c in loads[3:]:
+        c.wait()
+    cols_start(2, wgu, Dz)
+    rows_start(3, wd)
+    for i in (5, 6, 7):
+        ag_step(ag1, 0, i)
+    lax.fori_loop(5, T, prepare, 0)
+
     def forward_block(j, carry):
-        i = lax.rem(j + 6, T)
+        pair = j // 2
+        pair = pair + 3 * ((3 - pair) // 3) - 3 * (pair // 3)
+        i = 2 * pair + lax.rem(j, 2)
 
         @pl.when(j == 3)
         def _():
@@ -513,8 +543,7 @@
         def _():
             wave(1, 2)
 
-        rows, cols, seg_row, seg_col, alive, position = block_layout(i)
-        cos, sin = rope_rows(position, cols)
+        cos, sin = turns(i)
         pre = mm(ag1[i, 0:B, :], wqkv[...])
         qkpre[i] = pre[:, 0 : QT + HEAD]
         parts = []
@@ -526,10 +555,9 @@
         for n in range(3):
             rot[i, :, n * HEAD : (n + 1) * HEAD] = parts[n]
         rot[i, :, 3 * HEAD : 4 * HEAD] = v
-        allowed = ((seg_row == seg_col) & (cols <= rows) & alive) | (cols == rows)
+        mask = ag4[i, :, 0:B].astype(F32)
         for n in range(2):
-            scores = mm_nt(parts[n], parts[2]) * score_scale
-            scores = jnp.where(allowed, scores, NEG_FILL)
+            scores = mm_nt(parts[n], parts[2]) * score_scale + mask
             expd = jnp.exp(scores - jnp.max(scores, axis=1, keepdims=True))
             prob = (expd / jnp.sum(expd, axis=1, keepdims=True)).astype(BF)
             probs[i, n * B : (n + 1) * B, :] = prob
@@ -540,11 +568,11 @@
         def _():
             sib_send(st, 0, 0, i)
 
-        for when, p in ((2, 3), (5, 1), (7, 2)):
+        for when, p, first in ((2, 3, 1), (4, 1, 1), (6, 2, 1), (6, 1, 0), (7, 2, 0)):
 
             @pl.when(j == when)
             def _():
-                relay_send(st, 0, 0, p)
+                relay_send(st, 0, 0, p, first)
 
         return carry
 
@@ -552,7 +580,7 @@
     wave(2, 2)
     for i in (5, 6, 7):
         ag_step(ag3, 2, i)
-    hid = tokens + rs_total(st, 0, 0, 2)
+    hid = tokens + relay_total(st, 0, 0)
     relay_done(st, 0)
     hidden[...] = hid
     second_scale = lax.rsqrt(jnp.mean(hid * hid, axis=1, keepdims=True) + EPS)
@@ -591,6 +619,30 @@
 
     lax.fori_loop(0, D // step, grad_gu, 0)
 
+    def scatter(item, buf, slots_ref, cut):
+        def send(d, to, _):
+            at = pl.ds(pl.multiple_of(to * Dz, Dz), Dz)
+            remote(
+                buf.at[at, cut],
+                slots_ref.at[f, :, cut],
+                zg_s.at[item, 0, d],
+                zg_r.at[item, 0, d],
+                r,
+                to,
+            ).start()
+
+        others(send)
+
+    def scatter_total(item, buf, slots_ref, cut):
+        total = buf[own(Dz), cut].astype(F32)
+        others(lambda d, to, fs: wait_recv(slots_ref.at[fs, :, cut], zg_r.at[item, 0, d]))
+        for d in range(1, F):
+            total = total + slots_ref[lax.rem(f + d, F), :, cut].astype(F32)
+        buf[own(Dz), cut] = total.astype(BF)
+
+    def scatter_done(item, buf, cut):
+        others(lambda d, to, fs: wait_send(buf.at[own(Dz), cut], zg_s.at[item, 0, d]))
+
     def hop(item, buf, slots_ref, s, up, to):
         slot = s if up else s + (F - s) * (1 - (to - s + F - 1) // F)
         return remote(
@@ -699,9 +751,36 @@
         def _():
             wait_send(buf, zg_s.at[item, 0, 0])
 
+    all_q, all_kv = pl.ds(0, QT), pl.ds(QT, 2 * HEAD)
     hops_start(0, wgu, zr_gu)
+    ag_done(ag2, 1)
+
+    def down_block(i, carry):
+        ag2[i] = mm(actd[i, :, 0:FT], wd[...]).astype(BF)
+
+        @pl.when(lax.rem(i, 2) == 1)
+        def _():
+            sib_send(ag2, 2, 0, i)
+
+        return carry
+
+    lax.fori_loop(0, T, down_block, 0)
+    rows_done(3, wd)
+
+    def grad_down(m, carry):
+        at = pl.ds(pl.multiple_of(m * step, step), step)
+        total = mm_tn(actd[0, :, 0:FT], ag3[0, :, at])
+        for k in range(1, T):
+            total = total + mm_tn(actd[k, :, 0:FT], ag3[k, :, at])
+        wd[:, at] = total.astype(BF)
+        return carry
+
+    lax.fori_loop(0, D // step, grad_down, 0)
+
+    row_hops_start(1, wd, zr_d)
     d_out = jnp.where(live, cot_ref[...].astype(F32), 0.0)
     pre_two = rs_total(st, 1, 1)
+    hops_step(0, wgu, zr_gu, 1)
     rs_done(st, 1)
     hid = hidden[...]
     second_scale = lax.rsqrt(jnp.mean(hid * hid, axis=1, keepdims=True) + EPS)
@@ -715,48 +794,110 @@
     ag4[0] = d_hid.astype(BF)
     ag_start(ag4, 3)
 
-    ag_done(ag2, 1)
-
-    def down_block(i, carry):
-        ag2[i] = mm(actd[i, :, 0:FT], wd[...]).astype(BF)
-
-        @pl.when(lax.rem(i, 2) == 1)
-        def _():
-            sib_send(ag2, 2, 0, i)
-
-        return carry
-
-    lax.fori_loop(0, T, down_block, 0)
-    rows_done(3, wd)
-
-    def grad_down(m, carry):
-        at = pl.ds(pl.multiple_of(m * step, step), step)
-        total = mm_tn(actd[0, :, 0:FT], ag3[0, :, at])
-        for k in range(1, T):
-            total = total + mm_tn(actd[k, :, 0:FT], ag3[k, :, at])
-        wd[:, at] = total.astype(BF)
-        return carry
-
-    lax.fori_loop(0, D // step, grad_down, 0)
-
-    row_hops_start(1, wd, zr_d)
     ag_done(ag3, 2)
     ghead[...] = jnp.zeros_like(ghead)
 
+    def piece_at(item, out, rows, rank, cut=None):
+        u = unit(rank)
+        start, size = (0, rows) if cut is None else (cut * (rows // 2), rows // 2)
+        if item == 0:
+            return out.at[u, pl.ds(start, size), :]
+        if item > 2:
+            return out.at[u, pl.ds(start, size), all_q if item == 3 else all_kv]
+        first = pl.multiple_of(lax.rem(u, GPF) * rows + start, rows // 2)
+        return out.at[pl.ds(first, size), :]
+
+    def has(item, rank, fn):
+        if item in (0, 3, 4):
+            fn()
+        else:
+            pl.when(unit(rank) // GPF == f)(fn)
+
+    def fin_copy(item, src, dst, sem, to):
+        return remote(src, dst, fin_s.at[item, sem], fin_r.at[item, sem], to, f)
+
+    def fin_start(item, src, out, rows):
+        def go():
+            dst = piece_at(item, out, rows, t)
+            fin_copy(item, src, dst, 2, xn).start()
+            fin_copy(item, src, dst, 4, yn).start()
+            fin_copy(item, src, dst, 1, sib).start()
+            pltpu.make_async_copy(src, dst, fin_s.at[item, 0]).start()
+
+        has(item, t, go)
+
+    def fin_step(item, out, rows, k):
+        rank = flip(k)
+        full = piece_at(item, out, rows, rank)
+
+        def go():
+            if k < 6:
+                wait_recv(full, fin_r.at[item, k])
+                part = piece_at(item, out, rows, rank, k // 4)
+                fin_copy(item, part, part, 4 + k, yn if k == 2 else xn).start()
+            else:
+                wait_recv(piece_at(item, out, rows, rank, 0), fin_r.at[item, 6])
+                wait_recv(piece_at(item, out, rows, rank, 1), fin_r.at[item, 8])
+            fin_copy(item, full, full, k + 1, sib).start()
+
+        has(item, rank, go)
+
+    def fin_end(item, src, out, rows):
+        for k in (1, 3, 5, 7):
+            full = piece_at(item, out, rows, flip(k))
+            has(item, flip(k), lambda: wait_recv(full, fin_r.at[item, k]))
+
+        def mine():
+            for k in (1, 2, 4):
+                wait_send(src, fin_s.at[item, k])
+            pltpu.make_async_copy(src, piece_at(item, out, rows, t), fin_s.at[item, 0]).wait()
+
+        has(item, t, mine)
+        for k in (2, 4, 6):
+            full = piece_at(item, out, rows, flip(k))
+            part = piece_at(item, out, rows, flip(k), 0)
+
+            def passed():
+                wait_send(full, fin_s.at[item, k + 1])
+                if k < 6:
+                    wait_send(part, fin_s.at[item, 4 + k])
+
+            has(item, flip(k), passed)
+
+    gu_piece = wgu.at[own(Dz), :]
+    q_piece, kv_piece = wqkv.at[own(Dz), all_q], wqkv.at[own(Dz), all_kv]
+    go_piece = st.at[0]
+
+    def grad_out(m, carry):
+        at = pl.ds(pl.multiple_of(m * step, step), step)
+        total = mm_tn(att[0], ag4[0, :, at])
+        for k in range(1, T):
+            total = total + mm_tn(att[k], ag4[k, :, at])
+        st[0, :, at] = total.astype(BF)
+        return carry
+
     def backward_block(i, carry):
         ag_step(ag4, 3, i)
-        for n in range(1, min(F, 4)):
-
-            @pl.when(i == 2 * n)
-            def _():
+
+        @pl.when(i == 1)
+        def _():
+            if F > 2:
+                hops_step(0, wgu, zr_gu, 2)
+
+        @pl.when(i == 3)
+        def _():
+            row_hops_step(1, wd, zr_d, 1)
+            for n in range(3, F):
                 hops_step(0, wgu, zr_gu, n)
 
-            @pl.when(i == 2 * n + 1)
-            def _():
+        @pl.when(i == 7)
+        def _():
+            for n in range(2, F - 1):
                 row_hops_step(1, wd, zr_d, n)
-
-        rows, cols, _, _, _, position = block_layout(i)
-        cos, sin = rope_rows(position, cols)
+            lax.fori_loop(0, D // step, grad_out, 0)
+            row_hops_start(2, go_piece, zr_o)
+
+        cos, sin = turns(i)
         d_att = mm_nt(ag4[i], wo[...]).astype(BF)
         k_rot = rot[i, :, QT : QT + HEAD]
         v = rot[i, :, QT + HEAD : QT + 2 * HEAD]
@@ -796,33 +937,28 @@
         for n in range(4):
             rot[i, :, n * HEAD : (n + 1) * HEAD] = d_pre[n]
         ag3[i] = mm_nt(rot[i], wqkv[...]).astype(BF)
-        rs_step(ag3, 3, 1, i)
-        for when, p in ((4, 3), (6, 1), (7, 2)):
+        @pl.when(lax.rem(i, 2) == 1)
+        def _():
+            sib_send(ag3, 3, 1, i)
+
+        for when, p in ((4, 1), (6, 2)):
 
             @pl.when(i == when)
             def _():
-                relay_send(ag2, 2, 0, p)
+                relay_send(ag3, 3, 1, p, 1)
+
+        for when, p, first in ((4, 3, 1), (5, 1, 1), (6, 2, 1), (7, 1, 0), (7, 2, 0)):
+
+            @pl.when(i == when)
+            def _():
+                relay_send(ag2, 2, 0, p, first)
 
         return carry
 
     lax.fori_loop(0, T, backward_block, 0)
-    rs_send(ag3, 3, 1, 3)
-    for n in range(4, F):
-        hops_step(0, wgu, zr_gu, n)
-        row_hops_step(1, wd, zr_d, n)
+    relay_send(ag3, 3, 1, 3, 1)
     cols_done(0, wqkv, Dz)
     rows_done(1, wo)
-
-    def grad_out(m, carry):
-        at = pl.ds(pl.multiple_of(m * step, step), step)
-        total = mm_tn(att[0], ag4[0, :, at])
-        for k in range(1, T):
-            total = total + mm_tn(att[k], ag4[k, :, at])
-        wo[:, at] = total.astype(BF)
-        return carry
-
-    lax.fori_loop(0, D // step, grad_out, 0)
-    row_hops_start(2, wo, zr_o)
 
     def grad_qkv(m, carry):
         at = pl.ds(pl.multiple_of(m * step, step), step)
@@ -833,82 +969,20 @@
         return carry
 
     lax.fori_loop(0, D // step, grad_qkv, 0)
-    hops_start(3, wqkv, zr_qkv)
-
-    def piece_at(item, out, rows, rank, cut=None):
-        u = unit(rank)
-        start, size = (0, rows) if cut is None else (cut * (rows // 2), rows // 2)
-        if item in (0, 3):
-            return out.at[u, pl.ds(start, size), :]
-        first = pl.multiple_of(lax.rem(u, GPF) * rows + start, rows // 2)
-        return out.at[pl.ds(first, size), :]
-
-    def has(item, rank, fn):
-        if item in (0, 3):
-            fn()
-        else:
-            pl.when(unit(rank) // GPF == f)(fn)
-
-    def fin_copy(item, src, dst, sem, to):
-        return remote(src, dst, fin_s.at[item, sem], fin_r.at[item, sem], to, f)
-
-    def fin_start(item, src, out, rows):
-        def go():
-            dst = piece_at(item, out, rows, t)
-            fin_copy(item, src, dst, 2, xn).start()
-            fin_copy(item, src, dst, 4, yn).start()
-            fin_copy(item, src, dst, 1, sib).start()
-            pltpu.make_async_copy(src, dst, fin_s.at[item, 0]).start()
-
-        has(item, t, go)
-
-    def fin_step(item, out, rows, k):
-        rank = flip(k)
-        full = piece_at(item, out, rows, rank)
-
-        def go():
-            if k < 6:
-                wait_recv(full, fin_r.at[item, k])
-                part = piece_at(item, out, rows, rank, k // 4)
-                fin_copy(item, part, part, 4 + k, yn if k == 2 else xn).start()
-            else:
-                wait_recv(piece_at(item, out, rows, rank, 0), fin_r.at[item, 6])
-                wait_recv(piece_at(item, out, rows, rank, 1), fin_r.at[item, 8])
-            fin_copy(item, full, full, k + 1, sib).start()
-
-        has(item, rank, go)
-
-    def fin_end(item, src, out, rows):
-        for k in (1, 3, 5, 7):
-            full = piece_at(item, out, rows, flip(k))
-            has(item, flip(k), lambda: wait_recv(full, fin_r.at[item, k]))
-
-        def mine():
-            for k in (1, 2, 4):
-                wait_send(src, fin_s.at[item, k])
-            pltpu.make_async_copy(src, piece_at(item, out, rows, t), fin_s.at[item, 0]).wait()
-
-        has(item, t, mine)
-        for k in (2, 4, 6):
-            full = piece_at(item, out, rows, flip(k))
-            part = piece_at(item, out, rows, flip(k), 0)
-
-            def passed():
-                wait_send(full, fin_s.at[item, k + 1])
-                if k < 6:
-                    wait_send(part, fin_s.at[item, 4 + k])
-
-            has(item, flip(k), passed)
-
-    gu_piece, qkv_piece = wgu.at[own(Dz), :], wqkv.at[own(Dz), :]
+    scatter(3, wqkv, zr_qkv, all_q)
+    scatter(4, wqkv, zr_qkv, all_kv)
+    relay_send(ag3, 3, 1, 1, 0)
+    relay_send(ag3, 3, 1, 2, 0)
+
     hops_total(0, wgu, zr_gu)
     fin_start(0, gu_piece, ggu_out, Dz)
     row_hops_total(1, wd, zr_d)
     fin_start(1, wd, gd_out, FT)
-    hops_step(3, wqkv, zr_qkv, 1)
-    row_hops_step(2, wo, zr_o, 1)
-
-    pre_one = rs_total(ag3, 3, 1)
+    row_hops_step(2, go_piece, zr_o, 1)
+    for k in (2, 4):
+        fin_step(0, ggu_out, Dz, k)
+
+    pre_one = relay_total(ag3, 3, 1)
     tokens = tok_ref[...].astype(F32)
     first_scale = lax.rsqrt(jnp.mean(tokens * tokens, axis=1, keepdims=True) + EPS)
     first_hat = tokens * first_scale
@@ -930,19 +1004,15 @@
         remote(vz.at[f], vz.at[f], vz_s.at[d], vz_r.at[d], r, to).start()
 
     others(vec_send)
-    for n in range(2, F):
-        hops_step(3, wqkv, zr_qkv, n)
-        row_hops_step(2, wo, zr_o, n)
-        if n == 2:
-            for k in (2, 4):
-                fin_step(0, ggu_out, Dz, k)
-                fin_step(1, gd_out, FT, k)
-            out = hidden[...] + rs_total(ag2, 2, 0, 2)
-            mixed_out[...] = jnp.where(live, out, 0.0).astype(BF)
-    hops_total(3, wqkv, zr_qkv)
-    fin_start(3, qkv_piece, gqkv_out, Dz)
-    row_hops_total(2, wo, zr_o)
-    fin_start(2, wo, go_out, QT)
+    for n in range(2, F - 1):
+        row_hops_step(2, go_piece, zr_o, n)
+    fin_step(0, ggu_out, Dz, 6)
+    for k in (2, 4):
+        fin_step(1, gd_out, FT, k)
+    out = hidden[...] + relay_total(ag2, 2, 0)
+    mixed_out[...] = jnp.where(live, out, 0.0).astype(BF)
+    scatter_total(3, wqkv, zr_qkv, all_q)
+    fin_start(3, q_piece, gqkv_out, Dz)
 
     def vec_recv(d, to, fs):
         wait_recv(vz.at[fs], vz_r.at[d])
@@ -954,8 +1024,11 @@
     vp[t] = total
     for k in range(1, T):
         remote(vp.at[t], vp.at[t], vp_s.at[k], vp_r.at[k], base + flip(k), f).start()
-    fin_step(0, ggu_out, Dz, 6)
+    row_hops_total(2, go_piece, zr_o)
+    fin_start(2, go_piece, go_out, QT)
     fin_step(1, gd_out, FT, 6)
+    scatter_total(4, wqkv, zr_qkv, all_kv)
+    fin_start(4, kv_piece, gqkv_out, Dz)
     for k in range(1, T):
         wait_recv(vp.at[flip(k)], vp_r.at[k])
     total = vp[0]
@@ -969,19 +1042,22 @@
     for k in (2, 4, 6):
         fin_step(3, gqkv_out, Dz, k)
         fin_step(2, go_out, QT, k)
+        fin_step(4, gqkv_out, Dz, k)
     fin_end(0, gu_piece, ggu_out, Dz)
     fin_end(1, wd, gd_out, FT)
-    fin_end(3, qkv_piece, gqkv_out, Dz)
-    fin_end(2, wo, go_out, QT)
+    fin_end(3, q_piece, gqkv_out, Dz)
+    fin_end(2, go_piece, go_out, QT)
+    fin_end(4, kv_piece, gqkv_out, Dz)
 
     ag_done(ag1, 0)
     ag_done(ag4, 3)
     relay_done(ag2, 2)
-    rs_done(ag3, 3)
+    relay_done(ag3, 3)
     hops_done(0, wgu)
-    hops_done(3, wqkv)
+    scatter_done(3, wqkv, all_q)
+    scatter_done(4, wqkv, all_kv)
     row_hops_done(1, wd)
-    row_hops_done(2, wo)
+    row_hops_done(2, go_piece)
     for d in range(1, F):
         wait_send(normsb.at[0], nz_s.at[d])
         wait_send(vz.at[0], vz_s.at[d])
@@ -989,7 +1065,9 @@
         wait_send(vp.at[0], vp_s.at[k])
 
 
-def finish_kernel(scale, gqkv, ggu, go, gd, oq, ok, ov, og, ou, oo, od):
+def finish_kernel(
+    scale, gqkv, ggu, go, gd, vec, mixed, dtok, oq, ok, ov, og, ou, oo, od, o1, o2, oh, om, ot
+):
     x = gqkv[0].astype(F32) * scale
     w = oq.shape[1]
     oq[...] = x[:, 0:w]
@@ -1001,6 +1079,16 @@
     ou[...] = x[:, w : 2 * w]
     oo[...] = go[...].astype(F32) * scale
     od[...] = gd[...].astype(F32) * scale
+    om[...] = mixed[...]
+    ot[...] = dtok[...]
+
+    @pl.when(pl.program_id(0) == 0)
+    def _():
+        w = o1.shape[1]
+        o1[...] = vec[0:1, 0:w] * scale
+        o2[...] = vec[1:2, 0:w] * scale
+        oh[0:1, :] = vec[2:3, w : w + HEAD] * scale
+        oh[1:2, :] = vec[2:3, w + HEAD : w + 2 * HEAD] * scale
 
 
 def per_device(
@@ -1052,7 +1140,7 @@
             pltpu.VMEM((T, B, D), BF),
             pltpu.VMEM((T, B, D), BF),
             pltpu.VMEM((2, 4, B, D), BF),
-            pltpu.VMEM((2, 4, B, D), BF),
+            pltpu.VMEM((2, 3, B, D), BF),
             pltpu.VMEM((D, QT + 2 * HEAD), BF),
             pltpu.VMEM((D, 2 * FT), BF),
             pltpu.VMEM((QT, D), BF),
@@ -1068,25 +1156,26 @@
             pltpu.VMEM((F + 1, Dz, 2 * FT), BF),
             pltpu.VMEM((2, FT, D), BF),
             pltpu.VMEM((2, QT, D), BF),
-            pltpu.VMEM((F + 1, Dz, QT + 2 * HEAD), BF),
+            pltpu.VMEM((F, Dz, QT + 2 * HEAD), BF),
             pltpu.VMEM((F, 8, D), F32),
             pltpu.VMEM((T, 8, D), F32),
             pltpu.VMEM((8, HEAD), F32),
+            pltpu.VMEM((T, B, HEAD), F32),
             dma((4, 9)),
             dma((4, 9)),
             dma((4, 4)),
             dma((4, 4)),
-            dma((4, 4)),
-            dma((4, 4)),
+            dma((4, 6)),
+            dma((4, 6)),
             dma((4, 2, F)),
             dma((4, 2, F)),
             dma((F,)),
             dma((F,)),
             dma((8,)),
-            dma((4, 2, F)),
-            dma((4, 2, F)),
-            dma((4, 9)),
-            dma((4, 9)),
+            dma((5, 2, F)),
+            dma((5, 2, F)),
+            dma((5, 9)),
+            dma((5, 9)),
             dma((F,)),
             dma((F,)),
             dma((T,)),
@@ -1119,11 +1208,9 @@
         vec = lax.psum(vec, "rep", axis_index_groups=groups)
     scale = 1.0 / math.sqrt(B * T * G * F)
 
-    def order(u):
-        return u
-
     qb, fb = QZ // T, FZ // T
-    oq, ok, ov, og, ou, oo, od = pl.pallas_call(
+    bb = B // T
+    oq, ok, ov, og, ou, oo, od, o1, o2, oh, mixed, d_tokens = pl.pallas_call(
         functools.partial(finish_kernel, scale),
         grid=(T,),
         out_shape=(
@@ -1134,12 +1221,20 @@
             sds((Dz, FF), F32),
             sds((QZ, D), F32),
             sds((FZ, D), F32),
+            sds((1, Dz), F32),
+            sds((1, Dz), F32),
+            sds((2, HEAD), F32),
+            sds((B, D), BF),
+            sds((B, D), BF),
         ),
         in_specs=[
             pl.BlockSpec((1, Dz, QT + 2 * HEAD), lambda u: (u, 0, 0)),
             pl.BlockSpec((1, Dz, 2 * FT), lambda u: (u, 0, 0)),
             pl.BlockSpec((qb, D), lambda u: (u, 0)),
             pl.BlockSpec((fb, D), lambda u: (u, 0)),
+            pl.BlockSpec((8, Dz + 2 * HEAD), lambda u: (0, 0)),
+            pl.BlockSpec((bb, D), lambda u: (u, 0)),
+            pl.BlockSpec((bb, D), lambda u: (u, 0)),
         ],
         out_specs=(
             pl.BlockSpec((Dz, QT), lambda u: (0, u)),
@@ -1149,19 +1244,23 @@
             pl.BlockSpec((Dz, FT), lambda u: (0, u)),
             pl.BlockSpec((qb, D), lambda u: (u, 0)),
             pl.BlockSpec((fb, D), lambda u: (u, 0)),
+            pl.BlockSpec((1, Dz), lambda u: (0, 0)),
+            pl.BlockSpec((1, Dz), lambda u: (0, 0)),
+            pl.BlockSpec((2, HEAD), lambda u: (0, 0)),
+            pl.BlockSpec((bb, D), lambda u: (u, 0)),
+            pl.BlockSpec((bb, D), lambda u: (u, 0)),
         ),
-    )(gqkv, ggu, go, gd)
-    vec = vec * scale
+    )(gqkv, ggu, go, gd, vec, mixed, d_tokens)
     return (
         mixed,
         d_tokens,
-        vec[0, 0:Dz],
+        o1.reshape(Dz),
         oq,
         ok,
         ov,
-        jnp.concatenate([vec[2:3, Dz : Dz + HEAD], vec[2:3, Dz + HEAD : Dz + 2 * HEAD]], axis=0),
+        oh,
         oo,
-        vec[1, 0:Dz],
+        o2.reshape(Dz),
         og,
         ou,
         od,

time: 279 us -> 263 us (0.943)
  Pallas kernels: 272 us -> 260 us
    pallas_call x1, Pallas kernels: 263 us -> 249 us  [per_device(): pl.pallas_call(functools.partial(layer_kernel, F, B, D), out_shape=(sds((...]
where the time goes in v3:
time: 263 us; the launch traced here: 262 us
  Pallas kernels  260 us (99%)
    pallas_call x1, Pallas kernels, per_device(): pl.pallas_call(functools.partial(layer_kernel, F, B, D), out_shape=(sds((...  249 us
    pallas_call x1, Pallas kernels, per_device(): pl.pallas_call(functools.partial(finish_kernel, scale), grid=(T,), out_sh...  10.4 us

profile of v3, /device:TPU:9, one launch (start us, length us, event | category | flops | bytes accessed | tf_op | source)
XLA Modules:
  0.0 262.5 jit_solution(8550902056857374259)
XLA Ops:
  0.6 0.7 reshape.84
  1.3 0.7 convert.7
  2.0 0.0 copy-start
  2.0 0.6 copy-done
  2.6 249.3 %shard_map.229 = (bf16[8,256,512]{2,1,0:T(8,128)(2,1)}, bf16[8,256,768]{2,1,0:T(8,128)(2,1)}, bf16[512,1024]{1,0:T(8,128)(2,1)}, bf16[768,1024]{1,0:T(8,128)(2,1...) custom-call(bf16[256,1024]{1,0:T(8,128)(2,1)} %tok_ref.1, bf16[256,1024]{1,0:T(8,128)(2,1)} %cot_ref.1, ...), custom_call_target="tpu_custom_call" | custom-call | tf_op jit(solution)/shard_map/pallas_call | solution.py:1123
  251.9 10.4 %shard_map.230 = (f32[256,2048]{1,0:T(8,128)}, f32[256,1024]{1,0:T(8,128)}, f32[256,1024]{1,0:T(8,128)}, f32[256,3072]{1,0:T(8,128)}, f32[256,3072]{1,0:T(8,128)...) custom-call(bf16[8,256,512]{2,1,0:T(8,128)(2,1)} %get-tuple-element., ...), custom_call_target="tpu_custom_call" | custom-call | tf_op jit(solution)/shard_map/pallas_call | solution.py:1213
  (2 shorter events, 0.0 us)
Async XLA Ops:
  2.0 0.6 copy-start

commit v4 on v3

--- a/solution.py
+++ b/solution.py
@@ -534,11 +534,6 @@
         pair = pair + 3 * ((3 - pair) // 3) - 3 * (pair // 3)
         i = 2 * pair + lax.rem(j, 2)
 
-        @pl.when(j == 3)
-        def _():
-            for n in (1, 2, 3):
-                ag_step(ag3, 2, n)
-
         @pl.when(j == 4)
         def _():
             wave(1, 2)
@@ -559,7 +554,7 @@
         for n in range(2):
             scores = mm_nt(parts[n], parts[2]) * score_scale + mask
             expd = jnp.exp(scores - jnp.max(scores, axis=1, keepdims=True))
-            prob = (expd / jnp.sum(expd, axis=1, keepdims=True)).astype(BF)
+            prob = (expd * (1.0 / jnp.sum(expd, axis=1, keepdims=True))).astype(BF)
             probs[i, n * B : (n + 1) * B, :] = prob
             att[i, :, n * HEAD : (n + 1) * HEAD] = mm(prob, v).astype(BF)
         st[i] = mm(att[i], wo[...]).astype(BF)
@@ -577,15 +572,17 @@
         return carry
 
     lax.fori_loop(0, T, forward_block, 0)
+    for i in (1, 2, 3):
+        ag_step(ag3, 2, i)
     wave(2, 2)
-    for i in (5, 6, 7):
-        ag_step(ag3, 2, i)
     hid = tokens + relay_total(st, 0, 0)
     relay_done(st, 0)
     hidden[...] = hid
     second_scale = lax.rsqrt(jnp.mean(hid * hid, axis=1, keepdims=True) + EPS)
     ag2[0] = (hid * second_scale * gain_two).astype(BF)
     ag_start(ag2, 1)
+    for i in (5, 6, 7):
+        ag_step(ag3, 2, i)
     for m in range(3, F):
         wave(m, 2)
 
@@ -597,23 +594,33 @@
         silu = gate * sig
         actd[i, :, 0:FT] = (silu * up).astype(BF)
         d_act = mm_nt(ag3[i], wd[...])
-        actd[i, :, FT : 2 * FT] = (d_act * up * sig * (1.0 + gate * (1.0 - sig))).astype(BF)
+        actd[i, :, FT : 2 * FT] = (d_act * up * (sig + silu * (1.0 - sig))).astype(BF)
         actd[i, :, 2 * FT : 3 * FT] = (d_act * silu).astype(BF)
         st[i] = mm_nt(actd[i, :, FT : 3 * FT], wgu[...]).astype(BF)
-        rs_step(st, 1, 1, i)
+        @pl.when(lax.rem(i, 2) == 1)
+        def _():
+            sib_send(st, 1, 1, i)
+
+        for when, p in ((4, 1), (6, 2)):
+
+            @pl.when(i == when)
+            def _():
+                relay_send(st, 1, 1, p, 1)
+
         return carry
 
     lax.fori_loop(0, T, ffn_block, 0)
-    rs_send(st, 1, 1, 3)
+    relay_send(st, 1, 1, 3, 1)
     cols_done(2, wgu, Dz)
 
     step = 256
 
     def grad_gu(m, carry):
         at = pl.ds(pl.multiple_of(m * step, step), step)
-        total = mm_tn(ag2[0, :, at], actd[0, :, FT : 3 * FT])
-        for k in range(1, T):
-            total = total + mm_tn(ag2[k, :, at], actd[k, :, FT : 3 * FT])
+        left, right = ag2[:, :, at], actd[:, :, FT : 3 * FT]
+        total = mm_tn(
+            left.reshape(T * B, left.shape[2]), right.reshape(T * B, right.shape[2])
+        )
         wgu[at, :] = total.astype(BF)
         return carry
 
@@ -765,13 +772,16 @@
         return carry
 
     lax.fori_loop(0, T, down_block, 0)
+    relay_send(st, 1, 1, 1, 0)
+    relay_send(st, 1, 1, 2, 0)
     rows_done(3, wd)
 
     def grad_down(m, carry):
         at = pl.ds(pl.multiple_of(m * step, step), step)
-        total = mm_tn(actd[0, :, 0:FT], ag3[0, :, at])
-        for k in range(1, T):
-            total = total + mm_tn(actd[k, :, 0:FT], ag3[k, :, at])
+        left, right = actd[:, :, 0:FT], ag3[:, :, at]
+        total = mm_tn(
+            left.reshape(T * B, left.shape[2]), right.reshape(T * B, right.shape[2])
+        )
         wd[:, at] = total.astype(BF)
         return carry
 
@@ -779,9 +789,11 @@
 
     row_hops_start(1, wd, zr_d)
     d_out = jnp.where(live, cot_ref[...].astype(F32), 0.0)
-    pre_two = rs_total(st, 1, 1)
+    for p in (3, 1, 2):
+        relay_send(ag2, 2, 0, p, 1)
+    pre_two = relay_total(st, 1, 1)
     hops_step(0, wgu, zr_gu, 1)
-    rs_done(st, 1)
+    relay_done(st, 1)
     hid = hidden[...]
     second_scale = lax.rsqrt(jnp.mean(hid * hid, axis=1, keepdims=True) + EPS)
     second_hat = hid * second_scale
@@ -870,30 +882,42 @@
 
     def grad_out(m, carry):
         at = pl.ds(pl.multiple_of(m * step, step), step)
-        total = mm_tn(att[0], ag4[0, :, at])
-        for k in range(1, T):
-            total = total + mm_tn(att[k], ag4[k, :, at])
+        left, right = att[...], ag4[:, :, at]
+        total = mm_tn(
+            left.reshape(T * B, left.shape[2]), right.reshape(T * B, right.shape[2])
+        )
         st[0, :, at] = total.astype(BF)
         return carry
 
     def backward_block(i, carry):
         ag_step(ag4, 3, i)
 
-        @pl.when(i == 1)
+        @pl.when(i == 0)
         def _():
             if F > 2:
                 hops_step(0, wgu, zr_gu, 2)
 
-        @pl.when(i == 3)
-        def _():
-            row_hops_step(1, wd, zr_d, 1)
+        @pl.when(i == 2)
+        def _():
             for n in range(3, F):
                 hops_step(0, wgu, zr_gu, n)
 
-        @pl.when(i == 7)
+        @pl.when(i == 3)
+        def _():
+            row_hops_step(1, wd, zr_d, 1)
+
+        @pl.when(i == 6)
+        def _():
+            hops_total(0, wgu, zr_gu)
+            fin_start(0, gu_piece, ggu_out, Dz)
+
+        @pl.when(i == 6)
         def _():
             for n in range(2, F - 1):
                 row_hops_step(1, wd, zr_d, n)
+
+        @pl.when(i == 7)
+        def _():
             lax.fori_loop(0, D // step, grad_out, 0)
             row_hops_start(2, go_piece, zr_o)
 
@@ -947,7 +971,7 @@
             def _():
                 relay_send(ag3, 3, 1, p, 1)
 
-        for when, p, first in ((4, 3, 1), (5, 1, 1), (6, 2, 1), (7, 1, 0), (7, 2, 0)):
+        for when, p, first in ((3, 1, 0), (3, 2, 0)):
 
             @pl.when(i == when)
             def _():
@@ -962,9 +986,10 @@
 
     def grad_qkv(m, carry):
         at = pl.ds(pl.multiple_of(m * step, step), step)
-        total = mm_tn(ag1[0, 0:B, at], rot[0])
-        for k in range(1, T):
-            total = total + mm_tn(ag1[k, 0:B, at], rot[k])
+        left, right = ag1[:, 0:B, at], rot[...]
+        total = mm_tn(
+            left.reshape(T * B, left.shape[2]), right.reshape(T * B, right.shape[2])
+        )
         wqkv[at, :] = total.astype(BF)
         return carry
 
@@ -974,8 +999,6 @@
     relay_send(ag3, 3, 1, 1, 0)
     relay_send(ag3, 3, 1, 2, 0)
 
-    hops_total(0, wgu, zr_gu)
-    fin_start(0, gu_piece, ggu_out, Dz)
     row_hops_total(1, wd, zr_d)
     fin_start(1, wd, gd_out, FT)
     row_hops_step(2, go_piece, zr_o, 1)
@@ -1068,15 +1091,16 @@
 def finish_kernel(
     scale, gqkv, ggu, go, gd, vec, mixed, dtok, oq, ok, ov, og, ou, oo, od, o1, o2, oh, om, ot
 ):
-    x = gqkv[0].astype(F32) * scale
-    w = oq.shape[1]
-    oq[...] = x[:, 0:w]
-    ok[...] = x[:, w : w + HEAD]
-    ov[...] = x[:, w + HEAD : w + 2 * HEAD]
-    x = ggu[0].astype(F32) * scale
-    w = og.shape[1]
-    og[...] = x[:, 0:w]
-    ou[...] = x[:, w : 2 * w]
+    n = gqkv.shape[0]
+    w, v = oq.shape[1] // n, og.shape[1] // n
+    for i in range(n):
+        x = gqkv[i].astype(F32) * scale
+        oq[:, i * w : (i + 1) * w] = x[:, 0:w]
+        ok[:, i * HEAD : (i + 1) * HEAD] = x[:, w : w + HEAD]
+        ov[:, i * HEAD : (i + 1) * HEAD] = x[:, w + HEAD : w + 2 * HEAD]
+        x = ggu[i].astype(F32) * scale
+        og[:, i * v : (i + 1) * v] = x[:, 0:v]
+        ou[:, i * v : (i + 1) * v] = x[:, v : 2 * v]
     oo[...] = go[...].astype(F32) * scale
     od[...] = gd[...].astype(F32) * scale
     om[...] = mixed[...]
@@ -1208,11 +1232,13 @@
         vec = lax.psum(vec, "rep", axis_index_groups=groups)
     scale = 1.0 / math.sqrt(B * T * G * F)
 
-    qb, fb = QZ // T, FZ // T
-    bb = B // T
+    steps = 4
+    n = T // steps
+    qb, fb = QZ // steps, FZ // steps
+    bb = B // steps
     oq, ok, ov, og, ou, oo, od, o1, o2, oh, mixed, d_tokens = pl.pallas_call(
         functools.partial(finish_kernel, scale),
-        grid=(T,),
+        grid=(steps,),
         out_shape=(
             sds((Dz, QW), F32),
             sds((Dz, KW), F32),
@@ -1228,8 +1254,8 @@
             sds((B, D), BF),
         ),
         in_specs=[
-            pl.BlockSpec((1, Dz, QT + 2 * HEAD), lambda u: (u, 0, 0)),
-            pl.BlockSpec((1, Dz, 2 * FT), lambda u: (u, 0, 0)),
+            pl.BlockSpec((n, Dz, QT + 2 * HEAD), lambda u: (u, 0, 0)),
+            pl.BlockSpec((n, Dz, 2 * FT), lambda u: (u, 0, 0)),
             pl.BlockSpec((qb, D), lambda u: (u, 0)),
             pl.BlockSpec((fb, D), lambda u: (u, 0)),
             pl.BlockSpec((8, Dz + 2 * HEAD), lambda u: (0, 0)),
@@ -1237,11 +1263,11 @@
             pl.BlockSpec((bb, D), lambda u: (u, 0)),
         ],
         out_specs=(
-            pl.BlockSpec((Dz, QT), lambda u: (0, u)),
-            pl.BlockSpec((Dz, HEAD), lambda u: (0, u)),
-            pl.BlockSpec((Dz, HEAD), lambda u: (0, u)),
-            pl.BlockSpec((Dz, FT), lambda u: (0, u)),
-            pl.BlockSpec((Dz, FT), lambda u: (0, u)),
+            pl.BlockSpec((Dz, n * QT), lambda u: (0, u)),
+            pl.BlockSpec((Dz, n * HEAD), lambda u: (0, u)),
+            pl.BlockSpec((Dz, n * HEAD), lambda u: (0, u)),
+            pl.BlockSpec((Dz, n * FT), lambda u: (0, u)),
+            pl.BlockSpec((Dz, n * FT), lambda u: (0, u)),
             pl.BlockSpec((qb, D), lambda u: (u, 0)),
             pl.BlockSpec((fb, D), lambda u: (u, 0)),
             pl.BlockSpec((1, Dz), lambda u: (0, 0)),

time: 263 us -> 249 us (0.947)
  Pallas kernels: 260 us -> 246 us
    pallas_call x1, Pallas kernels: 249 us -> 236 us  [per_device(): pl.pallas_call(functools.partial(layer_kernel, F, B, D), out_shape=(sds((...]
where the time goes in v4:
time: 249 us; the launch traced here: 248 us
  Pallas kernels  246 us (99%)
    pallas_call x1, Pallas kernels, per_device(): pl.pallas_call(functools.partial(layer_kernel, F, B, D), out_shape=(sds((...  236 us
    pallas_call x1, Pallas kernels, per_device(): pl.pallas_call(functools.partial(finish_kernel, scale), grid=(steps,), ou...  9.97 us

profile of v4, /device:TPU:9, one launch (start us, length us, event | category | flops | bytes accessed | tf_op | source)
XLA Modules:
  0.0 248.4 jit_solution(14129337309443835075)
XLA Ops:
  0.6 0.7 reshape.84
  1.3 0.7 convert.7
  2.0 0.0 copy-start
  2.0 0.6 copy-done
  2.6 235.7 %shard_map.229 = (bf16[8,256,512]{2,1,0:T(8,128)(2,1)}, bf16[8,256,768]{2,1,0:T(8,128)(2,1)}, bf16[512,1024]{1,0:T(8,128)(2,1)}, bf16[768,1024]{1,0:T(8,128)(2,1...) custom-call(bf16[256,1024]{1,0:T(8,128)(2,1)} %tok_ref.1, bf16[256,1024]{1,0:T(8,128)(2,1)} %cot_ref.1, ...), custom_call_target="tpu_custom_call" | custom-call | tf_op jit(solution)/shard_map/pallas_call | solution.py:1147
  238.3 10.0 %shard_map.230 = (f32[256,2048]{1,0:T(8,128)}, f32[256,1024]{1,0:T(8,128)}, f32[256,1024]{1,0:T(8,128)}, f32[256,3072]{1,0:T(8,128)}, f32[256,3072]{1,0:T(8,128)...) custom-call(bf16[8,256,512]{2,1,0:T(8,128)(2,1)} %get-tuple-element., ...), custom_call_target="tpu_custom_call" | custom-call | tf_op jit(solution)/shard_map/pallas_call | solution.py:1239
  (2 shorter events, 0.0 us)
Async XLA Ops:
  2.0 0.6 copy-start

commit v5 on v4

--- a/solution.py
+++ b/solution.py
@@ -981,6 +981,8 @@
 
     lax.fori_loop(0, T, backward_block, 0)
     relay_send(ag3, 3, 1, 3, 1)
+    row_hops_total(1, wd, zr_d)
+    fin_start(1, wd, gd_out, FT)
     cols_done(0, wqkv, Dz)
     rows_done(1, wo)
 
@@ -999,8 +1001,6 @@
     relay_send(ag3, 3, 1, 1, 0)
     relay_send(ag3, 3, 1, 2, 0)
 
-    row_hops_total(1, wd, zr_d)
-    fin_start(1, wd, gd_out, FT)
     row_hops_step(2, go_piece, zr_o, 1)
     for k in (2, 4):
         fin_step(0, ggu_out, Dz, k)

time: 249 us -> 246 us (0.988)
  Pallas kernels: 246 us -> 243 us
    pallas_call x1, Pallas kernels: 236 us -> 233 us  [per_device(): pl.pallas_call(functools.partial(layer_kernel, F, B, D), out_shape=(sds((...]
where the time goes in v5:
time: 246 us; the launch traced here: 245 us
  Pallas kernels  243 us (99%)
    pallas_call x1, Pallas kernels, per_device(): pl.pallas_call(functools.partial(layer_kernel, F, B, D), out_shape=(sds((...  233 us
    pallas_call x1, Pallas kernels, per_device(): pl.pallas_call(functools.partial(finish_kernel, scale), grid=(steps,), ou...  9.97 us

profile of v5, /device:TPU:9, one launch (start us, length us, event | category | flops | bytes accessed | tf_op | source)
XLA Modules:
  0.0 245.3 jit_solution(6692524556018102183)
XLA Ops:
  0.6 0.7 reshape.84
  1.3 0.7 convert.7
  2.0 0.0 copy-start
  2.0 0.6 copy-done
  2.6 232.6 %shard_map.229 = (bf16[8,256,512]{2,1,0:T(8,128)(2,1)}, bf16[8,256,768]{2,1,0:T(8,128)(2,1)}, bf16[512,1024]{1,0:T(8,128)(2,1)}, bf16[768,1024]{1,0:T(8,128)(2,1...) custom-call(bf16[256,1024]{1,0:T(8,128)(2,1)} %tok_ref.1, bf16[256,1024]{1,0:T(8,128)(2,1)} %cot_ref.1, ...), custom_call_target="tpu_custom_call" | custom-call | tf_op jit(solution)/shard_map/pallas_call | solution.py:1147
  235.2 10.0 %shard_map.230 = (f32[256,2048]{1,0:T(8,128)}, f32[256,1024]{1,0:T(8,128)}, f32[256,1024]{1,0:T(8,128)}, f32[256,3072]{1,0:T(8,128)}, f32[256,3072]{1,0:T(8,128)...) custom-call(bf16[8,256,512]{2,1,0:T(8,128)(2,1)} %get-tuple-element., ...), custom_call_target="tpu_custom_call" | custom-call | tf_op jit(solution)/shard_map/pallas_call | solution.py:1239
  (2 shorter events, 0.0 us)
Async XLA Ops:
  2.0 0.6 copy-start
